TPU v7x, 32 devices: a whole 2x2x4 slice. The times are simulated.
32 devices in a mesh: lon: 8 (over y, x, core), lat: 4 (over z).
Axes of the slice: x: 2, y: 2, z: 4, core: 2. Of those that a mesh axis runs over, the one named last changes fastest.
Arguments:
- adj_tracer: float32 [2, 8, 256, 1024], P(None, None, 'lat', 'lon'), may hold values from -108 to 108
- zonal_flow: bfloat16 [2, 8, 256, 1024], P(None, None, 'lat', 'lon'), may hold values from -0.25 to 0.25
- meridional_flow: bfloat16 [2, 8, 256, 1024], P(None, None, 'lat', 'lon'), may hold values from -0.25 to 0.25
- depth: int32 [256, 1024], P('lat', 'lon'), may hold values from 0 to 8
- coupling: float32 [2, 8], replicated, may hold values from -1 to 1
- surface_diag: float32 [256, 1024], P('lat', 'lon'), may hold values from 0.02 to 0.5
Outputs:
- tracer_adjoint: float32 [2, 8, 256, 1024], P(None, None, 'lat', 'lon')
- surface_sens: float32 [256, 1024], P('lat', 'lon')
All inputs are finite; a program needn't handle non-finite values.
Results may differ from a plain program's by a relative error of at most 0.0003.
Values sent between devices are 32-bit elements; how exact they have to be, the bound alone decides.
No kernel may reach another device: no remote copies, remote signals or barrier semaphores. Data moves between devices by JAX's collectives and lax.ppermute only.
A program may use at most 64 MiB of HBM per device.

v0:
```python
import jax
import jax.numpy as jnp
from jax import lax
from jax.sharding import PartitionSpec as P

ITERS = 2


diffusion = 0.15


def padded(cells, sides, width, closed):
    for axis, dim in sides:
        count = lax.axis_size(axis)
        ends = count if closed else count - 1
        head = lax.slice_in_dim(cells, 0, width, axis=dim)
        tail = lax.slice_in_dim(cells, cells.shape[dim] - width, cells.shape[dim], axis=dim)
        cells = jnp.concatenate(
            [
                lax.ppermute(tail, axis, [(i, (i + 1) % count) for i in range(ends)]),
                cells,
                lax.ppermute(head, axis, [((i + 1) % count, i) for i in range(ends)]),
            ],
            axis=dim,
        )
    return cells


def helmholtz(surface, surface_diag):
    lon_ext = padded(surface, (("lon", 1),), 1, True)
    lat_ext = padded(surface, (("lat", 0),), 1, False)
    beside = lon_ext[:, :-2] + lon_ext[:, 2:] + lat_ext[:-2, :] + lat_ext[2:, :]
    return (surface_diag + 4.0) * surface - beside


def global_squares(residual):
    return lax.psum(jnp.sum(residual * residual), ("lon", "lat"))


def surface_solve(surface_rhs, surface_diag):
    surface_sol = jnp.zeros_like(surface_rhs)
    residual = surface_rhs
    direction = surface_rhs
    norm_now = global_squares(residual)
    for iteration in range(ITERS):
        image_field = helmholtz(direction, surface_diag)
        step_length = norm_now / lax.psum(jnp.sum(direction * image_field), ("lon", "lat"))
        surface_sol = surface_sol + step_length * direction
        residual = residual - step_length * image_field
        if iteration + 1 < ITERS:
            norm_next = global_squares(residual)
            direction = residual + norm_next / norm_now * direction
            norm_now = norm_next
    return surface_sol


def transpose_advect(middle, wet_cells, zonal_half, meridional_half, neighbours):
    adj_west, adj_east, adj_south, adj_north, wet_west, wet_east, wet_south, wet_north = neighbours
    flux_sum = wet_west * (zonal_half - diffusion) * (adj_west - middle)
    flux_sum = flux_sum + wet_east * (zonal_half + diffusion) * (middle - adj_east)
    flux_sum = flux_sum + wet_south * (meridional_half - diffusion) * (adj_south - middle)
    flux_sum = flux_sum + wet_north * (meridional_half + diffusion) * (middle - adj_north)
    return middle - wet_cells * flux_sum


def on_device(adj_tracer, zonal_flow, meridional_flow, depth, coupling, surface_diag):
    levels = lax.broadcasted_iota(jnp.int32, (adj_tracer.shape[1], 1, 1), 0)
    wet_cells = (levels < depth[None]).astype(jnp.float32)
    tracer_count = adj_tracer.shape[0]
    weights = coupling[:, :, None, None]
    adjoint = adj_tracer
    surface_sens = jnp.zeros(surface_diag.shape, jnp.float32)
    for instant in reversed(range(zonal_flow.shape[0])):
        masked = wet_cells[None] * adjoint
        surface_rhs = jnp.sum(weights * masked, axis=(0, 1))
        surface_sol = surface_solve(surface_rhs, surface_diag)
        surface_sens = surface_sens + surface_sol
        middle = masked + wet_cells[None] * weights * surface_sol[None, None]
        stacked = jnp.concatenate([middle, wet_cells[None]], axis=0)
        lon_ext = padded(stacked, (("lon", 3),), 1, True)
        lat_ext = padded(stacked, (("lat", 2),), 1, False)
        neighbours = (
            lon_ext[:tracer_count, :, :, :-2],
            lon_ext[:tracer_count, :, :, 2:],
            lat_ext[:tracer_count, :, :-2, :],
            lat_ext[:tracer_count, :, 2:, :],
            lon_ext[tracer_count, :, :, :-2],
            lon_ext[tracer_count, :, :, 2:],
            lat_ext[tracer_count, :, :-2, :],
            lat_ext[tracer_count, :, 2:, :],
        )
        zonal_half = 0.5 * zonal_flow[instant].astype(jnp.float32)
        meridional_half = 0.5 * meridional_flow[instant].astype(jnp.float32)
        adjoint = transpose_advect(middle, wet_cells, zonal_half, meridional_half, neighbours)
    return (adjoint, surface_sens)


def solution(mesh):
    in_specs = (
        P(None, None, "lat", "lon"),
        P(None, None, "lat", "lon"),
        P(None, None, "lat", "lon"),
        P("lat", "lon"),
        P(),
        P("lat", "lon"),
    )
    out_specs = (P(None, None, "lat", "lon"), P("lat", "lon"))
    return jax.shard_map(
        on_device, mesh=mesh, in_specs=in_specs, out_specs=out_specs, check_vma=False
    )
```

profile of v0, /device:TPU:0, one launch (start us, length us, event | category | flops | bytes accessed | tf_op | source)
XLA Modules:
  0.0 363.5 jit_solution(13173920956109177372)
XLA Ops:
  4.8 5.6 %collective-permute-start.2 = (f32[1,128]{0,1:T(8,128)S(1)}, f32[1,128]{0,1:T(8,128)S(1)}, u32[]{:S(2)}, u32[]{:S(2)}) collective-permute-start(f32[1,128]{0,1:T(8,128)S(1)} %get-tuple-element.66), channel_id=1, source_target_pairs={{0,1},{1,2},{2,3},{4,5},{5,6},{6,7},{8,9},{9,10},{10,11},{12,13},{... | collective-permute-start | bytes 1544 | tf_op jit(solution)/shard_map/ppermute | solution.py:20
  13.5 2.6 collective-permute-done
  16.8 39.7 %all-reduce.1 = (f32[]{:T(128)}, f32[]{:T(128)}) all-reduce(f32[]{:T(128)} %get-tuple-element.9, f32[]{:T(128)} %get-tuple-element.8), channel_id=1, replica_groups=mesh['lon'=8,'lat'=4] {'lon','lat'}, use_global_device_ids=true, to_apply=%region_2.0 | all-reduce | flops 2 | bytes 16 | tf_op jit(solution)/shard_map/psum | solution.py:37
  59.1 39.1 %psum.58 = f32[]{:T(128)} all-reduce(f32[]{:T(128)} %multiply_reduce_fusion.5), channel_id=1, replica_groups=mesh['lon'=8,'lat'=4] {'lon','lat'}, use_global_device_ids=true, to_apply=%region_6.0 | all-reduce | flops 1 | bytes 8 | tf_op jit(solution)/shard_map/psum | solution.py:37
  101.0 4.5 %collective-permute-start.6 = (f32[1,128]{0,1:T(8,128)S(1)}, f32[1,128]{0,1:T(8,128)S(1)}, u32[]{:S(2)}, u32[]{:S(2)}) collective-permute-start(f32[1,128]{0,1:T(8,128)S(1)} %get-tuple-element.62), channel_id=1, source_target_pairs={{0,1},{1,2},{2,3},{4,5},{5,6},{6,7},{8,9},{9,10},{10,11},{12,13},{... | collective-permute-start | bytes 1544 | tf_op jit(solution)/shard_map/ppermute | solution.py:20
  107.5 2.9 collective-permute-done.4
  112.0 39.9 %psum.59 = f32[]{:T(128)} all-reduce(f32[]{:T(128)} %fusion.54), channel_id=1, replica_groups=mesh['lon'=8,'lat'=4] {'lon','lat'}, use_global_device_ids=true, to_apply=%region_8.0 | all-reduce | flops 1 | bytes 8 | tf_op jit(solution)/shard_map/psum | solution.py:47
  154.0 2.6 collective-permute-start.9
  158.8 2.5 copy.23
  161.3 3.6 %collective-permute-start.10 = (f32[3,8,1,128]{3,1,2,0:T(8,128)}, f32[3,8,1,128]{3,1,2,0:T(8,128)}, u32[]{:S(2)}, u32[]{:S(2)}) collective-permute-start(f32[3,8,1,128]{3,1,2,0:T(8,128)} %copy.23), channel_id=1, source_target_pairs={{0,1},{1,2},{2,3},{4,5},{5,6},{6,7},{8,9},{9,10},{10,11},{12,13},{... | collective-permute-start | bytes 36872 | tf_op jit(solution)/shard_map/ppermute | solution.py:20
  164.9 2.5 copy.26
  176.9 2.9 fusion.8
  184.9 5.2 %collective-permute-start.14 = (f32[1,128]{0,1:T(8,128)S(1)}, f32[1,128]{0,1:T(8,128)S(1)}, u32[]{:S(2)}, u32[]{:S(2)}) collective-permute-start(f32[1,128]{0,1:T(8,128)S(1)} %get-tuple-element.58), channel_id=1, source_target_pairs={{0,1},{1,2},{2,3},{4,5},{5,6},{6,7},{8,9},{9,10},{10,11},{12,13},{... | collective-permute-start | bytes 1544 | tf_op jit(solution)/shard_map/ppermute | solution.py:20
  191.5 2.6 collective-permute-done.12
  194.8 40.5 %all-reduce = (f32[]{:T(128)}, f32[]{:T(128)}) all-reduce(f32[]{:T(128)} %get-tuple-element.7, f32[]{:T(128)} %get-tuple-element.6), channel_id=1, replica_groups=mesh['lon'=8,'lat'=4] {'lon','lat'}, use_global_device_ids=true, to_apply=%region_11.0 | all-reduce | flops 2 | bytes 16 | tf_op jit(solution)/shard_map/psum | solution.py:37
  237.3 40.3 %psum.62 = f32[]{:T(128)} all-reduce(f32[]{:T(128)} %multiply_reduce_fusion.2), channel_id=1, replica_groups=mesh['lon'=8,'lat'=4] {'lon','lat'}, use_global_device_ids=true, to_apply=%region_15.0 | all-reduce | flops 1 | bytes 8 | tf_op jit(solution)/shard_map/psum | solution.py:37
  280.3 4.6 %collective-permute-start.18 = (f32[1,128]{0,1:T(8,128)S(1)}, f32[1,128]{0,1:T(8,128)S(1)}, u32[]{:S(2)}, u32[]{:S(2)}) collective-permute-start(f32[1,128]{0,1:T(8,128)S(1)} %get-tuple-element.54), channel_id=1, source_target_pairs={{0,1},{1,2},{2,3},{4,5},{5,6},{6,7},{8,9},{9,10},{10,11},{12,13},{... | collective-permute-start | bytes 1544 | tf_op jit(solution)/shard_map/ppermute | solution.py:20
  287.1 2.6 collective-permute-done.16
  291.3 39.9 %psum.63 = f32[]{:T(128)} all-reduce(f32[]{:T(128)} %fusion.44), channel_id=1, replica_groups=mesh['lon'=8,'lat'=4] {'lon','lat'}, use_global_device_ids=true, to_apply=%region_17.0 | all-reduce | flops 1 | bytes 8 | tf_op jit(solution)/shard_map/psum | solution.py:47
  334.6 2.6 collective-permute-start.21
  339.4 2.5 copy.29
  341.9 2.5 collective-permute-start.22
  344.5 2.5 copy.32
  357.1 2.9 fusion.9
  (130 shorter events, 57.4 us)
Async XLA Ops:
  3.5 12.6 %collective-permute-start.3 = (f32[1,128]{0,1:T(8,128)S(1)}, f32[1,128]{0,1:T(8,128)S(1)}, u32[]{:S(2)}, u32[]{:S(2)}) collective-permute-start(f32[1,128]{0,1:T(8,128)S(1)} %get-tuple-element.67), channel_id=1, source_target_pairs={{1,0},{2,1},{3,2},{5,4},{6,5},{7,6},{9,8},{10,9},{11,10},{13,12},{... | collective-permute-start | bytes 1544 | tf_op jit(solution)/shard_map/ppermute | solution.py:22
  4.8 11.3 %collective-permute-start.2 = (f32[1,128]{0,1:T(8,128)S(1)}, f32[1,128]{0,1:T(8,128)S(1)}, u32[]{:S(2)}, u32[]{:S(2)}) collective-permute-start(f32[1,128]{0,1:T(8,128)S(1)} %get-tuple-element.66), channel_id=1, source_target_pairs={{0,1},{1,2},{2,3},{4,5},{5,6},{6,7},{8,9},{9,10},{10,11},{12,13},{... | collective-permute-start | bytes 1544 | tf_op jit(solution)/shard_map/ppermute | solution.py:20
  10.4 3.1 collective-permute-start.1
  12.2 3.9 %collective-permute-start = (f32[64,1]{0,1:T(1,128)S(1)}, f32[64,1]{0,1:T(1,128)S(1)}, u32[]{:S(2)}, u32[]{:S(2)}) collective-permute-start(f32[64,1]{0,1:T(1,128)S(1)} %get-tuple-element.64), channel_id=1, source_target_pairs={{0,4},{4,8},{8,12},{12,16},{16,20},{20,24},{24,28},{28,0},{1,5},{5... | collective-permute-start | bytes 776 | tf_op jit(solution)/shard_map/ppermute | solution.py:20
  99.7 10.7 %collective-permute-start.7 = (f32[1,128]{0,1:T(8,128)S(1)}, f32[1,128]{0,1:T(8,128)S(1)}, u32[]{:S(2)}, u32[]{:S(2)}) collective-permute-start(f32[1,128]{0,1:T(8,128)S(1)} %get-tuple-element.63), channel_id=1, source_target_pairs={{1,0},{2,1},{3,2},{5,4},{6,5},{7,6},{9,8},{10,9},{11,10},{13,12},{... | collective-permute-start | bytes 1544 | tf_op jit(solution)/shard_map/ppermute | solution.py:22
  101.0 9.4 %collective-permute-start.6 = (f32[1,128]{0,1:T(8,128)S(1)}, f32[1,128]{0,1:T(8,128)S(1)}, u32[]{:S(2)}, u32[]{:S(2)}) collective-permute-start(f32[1,128]{0,1:T(8,128)S(1)} %get-tuple-element.62), channel_id=1, source_target_pairs={{0,1},{1,2},{2,3},{4,5},{5,6},{6,7},{8,9},{9,10},{10,11},{12,13},{... | collective-permute-start | bytes 1544 | tf_op jit(solution)/shard_map/ppermute | solution.py:20
  105.5 1.9 collective-permute-start.5
  106.2 4.2 %collective-permute-start.4 = (f32[64,1]{0,1:T(1,128)S(1)}, f32[64,1]{0,1:T(1,128)S(1)}, u32[]{:S(2)}, u32[]{:S(2)}) collective-permute-start(f32[64,1]{0,1:T(1,128)S(1)} %get-tuple-element.60), channel_id=1, source_target_pairs={{0,4},{4,8},{8,12},{12,16},{16,20},{20,24},{24,28},{28,0},{1,5},{5... | collective-permute-start | bytes 776 | tf_op jit(solution)/shard_map/ppermute | solution.py:20
  154.0 14.8 %collective-permute-start.8 = (f32[3,8,64,1]{2,1,3,0:T(8,128)}, f32[3,8,64,1]{2,1,3,0:T(8,128)}, u32[]{:S(2)}, u32[]{:S(2)}) collective-permute-start(f32[3,8,64,1]{2,1,3,0:T(8,128)} %get-tuple-element.19), channel_id=1, source_target_pairs={{0,4},{4,8},{8,12},{12,16},{16,20},{20,24},{24,28},{28,0},{1,5},{5... | collective-permute-start | bytes 18440 | tf_op jit(solution)/shard_map/ppermute | solution.py:20
  154.0 14.9 %collective-permute-start.9 = (f32[3,8,64,1]{2,1,3,0:T(8,128)}, f32[3,8,64,1]{2,1,3,0:T(8,128)}, u32[]{:S(2)}, u32[]{:S(2)}) collective-permute-start(f32[3,8,64,1]{2,1,3,0:T(8,128)} %get-tuple-element.32), channel_id=1, source_target_pairs={{4,0},{8,4},{12,8},{16,12},{20,16},{24,20},{28,24},{0,28},{5,1},{9... | collective-permute-start | bytes 18440 | tf_op jit(solution)/shard_map/ppermute | solution.py:22
  161.3 10.8 %collective-permute-start.10 = (f32[3,8,1,128]{3,1,2,0:T(8,128)}, f32[3,8,1,128]{3,1,2,0:T(8,128)}, u32[]{:S(2)}, u32[]{:S(2)}) collective-permute-start(f32[3,8,1,128]{3,1,2,0:T(8,128)} %copy.23), channel_id=1, source_target_pairs={{0,1},{1,2},{2,3},{4,5},{5,6},{6,7},{8,9},{9,10},{10,11},{12,13},{... | collective-permute-start | bytes 36872 | tf_op jit(solution)/shard_map/ppermute | solution.py:20
  167.4 7.1 %collective-permute-start.11 = (f32[3,8,1,128]{3,1,2,0:T(8,128)}, f32[3,8,1,128]{3,1,2,0:T(8,128)}, u32[]{:S(2)}, u32[]{:S(2)}) collective-permute-start(f32[3,8,1,128]{3,1,2,0:T(8,128)} %copy.26), channel_id=1, source_target_pairs={{1,0},{2,1},{3,2},{5,4},{6,5},{7,6},{9,8},{10,9},{11,10},{13,12},{... | collective-permute-start | bytes 36872 | tf_op jit(solution)/shard_map/ppermute | solution.py:22
  183.5 10.6 %collective-permute-start.15 = (f32[1,128]{0,1:T(8,128)S(1)}, f32[1,128]{0,1:T(8,128)S(1)}, u32[]{:S(2)}, u32[]{:S(2)}) collective-permute-start(f32[1,128]{0,1:T(8,128)S(1)} %get-tuple-element.59), channel_id=1, source_target_pairs={{1,0},{2,1},{3,2},{5,4},{6,5},{7,6},{9,8},{10,9},{11,10},{13,12},{... | collective-permute-start | bytes 1544 | tf_op jit(solution)/shard_map/ppermute | solution.py:22
  184.9 9.2 %collective-permute-start.14 = (f32[1,128]{0,1:T(8,128)S(1)}, f32[1,128]{0,1:T(8,128)S(1)}, u32[]{:S(2)}, u32[]{:S(2)}) collective-permute-start(f32[1,128]{0,1:T(8,128)S(1)} %get-tuple-element.58), channel_id=1, source_target_pairs={{0,1},{1,2},{2,3},{4,5},{5,6},{6,7},{8,9},{9,10},{10,11},{12,13},{... | collective-permute-start | bytes 1544 | tf_op jit(solution)/shard_map/ppermute | solution.py:20
  190.1 1.4 collective-permute-start.13
  190.2 3.9 %collective-permute-start.12 = (f32[64,1]{0,1:T(1,128)S(1)}, f32[64,1]{0,1:T(1,128)S(1)}, u32[]{:S(2)}, u32[]{:S(2)}) collective-permute-start(f32[64,1]{0,1:T(1,128)S(1)} %get-tuple-element.56), channel_id=1, source_target_pairs={{0,4},{4,8},{8,12},{12,16},{16,20},{20,24},{24,28},{28,0},{1,5},{5... | collective-permute-start | bytes 776 | tf_op jit(solution)/shard_map/ppermute | solution.py:20
  279.0 10.6 %collective-permute-start.19 = (f32[1,128]{0,1:T(8,128)S(1)}, f32[1,128]{0,1:T(8,128)S(1)}, u32[]{:S(2)}, u32[]{:S(2)}) collective-permute-start(f32[1,128]{0,1:T(8,128)S(1)} %get-tuple-element.55), channel_id=1, source_target_pairs={{1,0},{2,1},{3,2},{5,4},{6,5},{7,6},{9,8},{10,9},{11,10},{13,12},{... | collective-permute-start | bytes 1544 | tf_op jit(solution)/shard_map/ppermute | solution.py:22
  280.3 9.3 %collective-permute-start.18 = (f32[1,128]{0,1:T(8,128)S(1)}, f32[1,128]{0,1:T(8,128)S(1)}, u32[]{:S(2)}, u32[]{:S(2)}) collective-permute-start(f32[1,128]{0,1:T(8,128)S(1)} %get-tuple-element.54), channel_id=1, source_target_pairs={{0,1},{1,2},{2,3},{4,5},{5,6},{6,7},{8,9},{9,10},{10,11},{12,13},{... | collective-permute-start | bytes 1544 | tf_op jit(solution)/shard_map/ppermute | solution.py:20
  284.9 2.2 collective-permute-start.17
  285.8 3.9 %collective-permute-start.16 = (f32[64,1]{0,1:T(1,128)S(1)}, f32[64,1]{0,1:T(1,128)S(1)}, u32[]{:S(2)}, u32[]{:S(2)}) collective-permute-start(f32[64,1]{0,1:T(1,128)S(1)} %get-tuple-element.52), channel_id=1, source_target_pairs={{0,4},{4,8},{8,12},{12,16},{16,20},{20,24},{24,28},{28,0},{1,5},{5... | collective-permute-start | bytes 776 | tf_op jit(solution)/shard_map/ppermute | solution.py:20
  334.6 14.4 %collective-permute-start.20 = (f32[3,8,64,1]{2,1,3,0:T(8,128)}, f32[3,8,64,1]{2,1,3,0:T(8,128)S(1)}, u32[]{:S(2)}, u32[]{:S(2)}) collective-permute-start(f32[3,8,64,1]{2,1,3,0:T(8,128)} %get-tuple-element.38), channel_id=1, source_target_pairs={{0,4},{4,8},{8,12},{12,16},{16,20},{20,24},{24,28},{28,0},{1,5},{5... | collective-permute-start | bytes 18440 | tf_op jit(solution)/shard_map/ppermute | solution.py:20
  334.6 14.4 %collective-permute-start.21 = (f32[3,8,64,1]{2,1,3,0:T(8,128)}, f32[3,8,64,1]{2,1,3,0:T(8,128)}, u32[]{:S(2)}, u32[]{:S(2)}) collective-permute-start(f32[3,8,64,1]{2,1,3,0:T(8,128)} %get-tuple-element.39), channel_id=1, source_target_pairs={{4,0},{8,4},{12,8},{16,12},{20,16},{24,20},{28,24},{0,28},{5,1},{9... | collective-permute-start | bytes 18440 | tf_op jit(solution)/shard_map/ppermute | solution.py:22
  341.9 10.3 %collective-permute-start.22 = (f32[3,8,1,128]{3,1,2,0:T(8,128)}, f32[3,8,1,128]{3,1,2,0:T(8,128)}, u32[]{:S(2)}, u32[]{:S(2)}) collective-permute-start(f32[3,8,1,128]{3,1,2,0:T(8,128)} %copy.29), channel_id=1, source_target_pairs={{0,1},{1,2},{2,3},{4,5},{5,6},{6,7},{8,9},{9,10},{10,11},{12,13},{... | collective-permute-start | bytes 36872 | tf_op jit(solution)/shard_map/ppermute | solution.py:20
  347.0 7.7 %collective-permute-start.23 = (f32[3,8,1,128]{3,1,2,0:T(8,128)}, f32[3,8,1,128]{3,1,2,0:T(8,128)}, u32[]{:S(2)}, u32[]{:S(2)}) collective-permute-start(f32[3,8,1,128]{3,1,2,0:T(8,128)} %copy.32), channel_id=1, source_target_pairs={{1,0},{2,1},{3,2},{5,4},{6,5},{7,6},{9,8},{10,9},{11,10},{13,12},{... | collective-permute-start | bytes 36872 | tf_op jit(solution)/shard_map/ppermute | solution.py:22
  (22 other events, 571.1 us)
where the time goes:
time: 366 us; the launch traced here: 363 us
  blocking collectives  239 us (65%)
  starting transfers between devices  43.2 us (12%)
  local copies, waits for them, and re-layouts  32.5 us (9%)
  other arithmetic  25.3 us (7%)
  waiting for transfers between devices  14.1 us (4%)
  between operations  9 us (2%)
    psum x4, blocking collectives, global_squares(): return lax.psum(jnp.sum(residual * residual), ('lon', 'lat'))  160 us
    psum x2, blocking collectives, surface_solve(): lax.psum(jnp.sum(direction * image_field), ('lon', 'lat'))  79.7 us
    ppermute x12, starting transfers between devices, padded(): lax.ppermute(tail, axis, [(i, (i + 1) % count) for i in range(ends)])  26.5 us
    ppermute x12, starting transfers between devices, padded(): lax.ppermute(head, axis, [((i + 1) % count, i) for i in range(ends)])  16.6 us
    unnamed x53, local copies, waits for them, and re-layouts  11.3 us
    ppermute x12, waiting for transfers between devices, padded(): lax.ppermute(tail, axis, [(i, (i + 1) % count) for i in range(ends)])  10.7 us
    concatenate x4, other arithmetic, padded(): jnp.concatenate([lax.ppermute(tail, axis, [(i, (i + 1) % count) for i in...  7.7 us
  transfers between devices with their start and end apart: 24, of which 8 were waited for; matrix products, arithmetic and copies ran while one was open for 7% of the time, Pallas kernels for 0%

commit v1 on v0

v1 whole, which is shorter than its diff:
```python
import jax
import jax.numpy as jnp
from jax import lax
from jax.experimental import pallas as pl
from jax.experimental.pallas import tpu as pltpu
from jax.sharding import PartitionSpec as P

DIFF = 0.15
SHIFT = 4.0
LANES = 128
ROWS = 64
HALO = 8
EXT = ROWS + 2 * HALO
PAD = EXT + 2 * HALO
CHUNKS = EXT // 8
FLOW_AT, MASK_AT, DEPTH_AT, DIAG_AT, MSG_ROWS = 8, 40, 104, 108, 120
DEP, DIA, B, H, U, V, W, HU, HV, HW = range(10)
PAIRS = ((0, 0), (0, 1), (0, 2), (1, 1), (1, 2), (2, 2))
NSUMS = 4 + 4 * len(PAIRS)


def lane_iota():
    return lax.broadcasted_iota(jnp.int32, (8, LANES), 1)


def roll(x, by):
    by = by % LANES
    return pltpu.roll(x, by, 1) if by else x


def over_groups(x):
    for by in (8, 16, 32, 64):
        x = x + roll(x, by)
    return x


def in_every_group(x, group):
    lane = lane_iota()
    return over_groups(jnp.where(lane // 8 == group, x, 0.0))


def level_rows(ref, at, count, index, south):
    start = at + count * index
    return ref[pl.ds(start - (8 - count) if south else start, 8), :]


def row_messages(coupling_free_refs):
    adj_ref, zon_ref, mer_ref, depth_ref, diag_ref, a_ref, b_ref = coupling_free_refs
    even = lax.rem(lax.axis_index("lat"), 2) == 0
    zero = jnp.zeros((8, LANES), jnp.float32)
    for ref in (a_ref, b_ref):
        ref[0:8, :] = zero
        ref[MSG_ROWS - 8 : MSG_ROWS, :] = zero

    def put(at, low, high):
        count = low.shape[0]
        a_ref[pl.ds(at, count), :] = jnp.where(even, high, low)
        b_ref[pl.ds(at, count), :] = jnp.where(even, low, high)

    depth_low = depth_ref[0:4, :].astype(jnp.float32)
    depth_high = depth_ref[ROWS - 4 : ROWS, :].astype(jnp.float32)
    for level in range(16):
        k = float(level % 8)
        low = jnp.where(depth_low > k, adj_ref[level, 0:4, :], 0.0)
        high = jnp.where(depth_high > k, adj_ref[level, ROWS - 4 : ROWS, :], 0.0)
        put(MASK_AT + 4 * level, low, high)
    put(DEPTH_AT, depth_low, depth_high)
    put(DIAG_AT, diag_ref[0:4, :], diag_ref[ROWS - 4 : ROWS, :])
    for which, ref in enumerate((zon_ref, mer_ref)):
        for k in range(8):
            low = 0.5 * ref[0, k, 0:16, :].astype(jnp.float32)
            high = 0.5 * ref[0, k, ROWS - 16 : ROWS, :].astype(jnp.float32)
            put(FLOW_AT + 2 * (8 * which + k), low[0:2], high[14:16])


def row_message_kernel(*refs):
    row_messages(refs)


def sort_rows(recv_a_ref, recv_b_ref, south_ref, north_ref, last):
    lat = lax.axis_index("lat")
    even = lax.rem(lat, 2) == 0
    for start in range(0, MSG_ROWS, 8):
        a = recv_a_ref[pl.ds(start, 8), :]
        b = recv_b_ref[pl.ds(start, 8), :]
        south_ref[pl.ds(start, 8), :] = jnp.where(lat == 0, 0.0, jnp.where(even, b, a))
        north_ref[pl.ds(start, 8), :] = jnp.where(lat == last, 0.0, jnp.where(even, a, b))


def make_pack_kernel(last):
    def kernel(adj_ref, zon_ref, mer_ref, depth_ref, diag_ref, ra_ref, rb_ref, o_ref, south_ref, north_ref):
        sort_rows(ra_ref, rb_ref, south_ref, north_ref, last)

        def group_of(shape):
            return lax.broadcasted_iota(jnp.int32, shape, 1) // 8

        group = group_of((ROWS, LANES))
        depth = depth_ref[...].astype(jnp.float32)
        packed = jnp.zeros((ROWS, LANES), jnp.float32)
        for level in range(16):
            value = jnp.where(depth > float(level % 8), adj_ref[level], 0.0)
            packed = jnp.where(group == level, roll(value, 8 * level + 4), packed)
        o_ref[HALO : HALO + ROWS, :] = packed
        for which, ref in enumerate((zon_ref, mer_ref)):
            for k in range(8):
                level = 8 * which + k
                value = 0.5 * ref[0, k].astype(jnp.float32)
                packed = jnp.where(group == level, roll(value, 8 * level + 4), packed)
        o_ref[EXT + HALO : EXT + HALO + ROWS, :] = packed
        packed = jnp.where(group == 0, roll(depth, 4), roll(diag_ref[...], 12))
        o_ref[2 * EXT + HALO : 2 * EXT + HALO + ROWS, :] = packed
        group = group_of((8, LANES))
        for ref, south, base in ((south_ref, True, 0), (north_ref, False, HALO + ROWS)):
            packed = jnp.zeros((8, LANES), jnp.float32)
            for level in range(16):
                value = level_rows(ref, MASK_AT, 4, level, south)
                packed = jnp.where(group == level, roll(value, 8 * level + 4), packed)
            o_ref[base : base + 8, :] = packed
            for level in range(16):
                value = level_rows(ref, FLOW_AT, 2, level, south)
                packed = jnp.where(group == level, roll(value, 8 * level + 4), packed)
            o_ref[EXT + base : EXT + base + 8, :] = packed
            dep = level_rows(ref, DEPTH_AT, 4, 0, south)
            dia = level_rows(ref, DIAG_AT, 4, 0, south)
            packed = jnp.where(group == 0, roll(dep, 4), roll(dia, 12))
            o_ref[2 * EXT + base : 2 * EXT + base + 8, :] = packed

    return kernel


def make_fields_kernel(last, devices):
    def kernel(
        c_ref, adj_ref, zon_ref, mer_ref, depth_ref, diag_ref, ra_ref, rb_ref, o_ref, pa_ref, pb_ref,
        am_ref, pq_ref, f_out_ref, z_out_ref, sums_ref,
        south_ref, north_ref, m_ref, f_ref, s_ref, sm_ref, sf_ref,
    ):
        lane = lane_iota()
        pos = lane % 8
        group = lane // 8
        inner = pos < 4
        level_of = (group % 8).astype(jnp.float32)
        lat = lax.axis_index("lat")
        even_lon = lax.rem(lax.axis_index("lon"), 2) == 0
        coup = [c_ref[level // 8, level % 8] for level in range(16)]
        square = [coup[k] * coup[k] + coup[k + 8] * coup[k + 8] for k in range(8)]
        coup_lane = jnp.zeros((8, LANES), jnp.float32)
        for level in range(16):
            coup_lane = jnp.where(group == level, coup[level], coup_lane)
        square_lane = coup_lane * coup_lane

        sort_rows(ra_ref, rb_ref, south_ref, north_ref, last)
        depth = depth_ref[...].astype(jnp.float32)
        lo, hi = HALO, HALO + EXT - 8
        mid = 2 * HALO
        for level in range(16):
            m_ref[level, mid : mid + ROWS, :] = jnp.where(depth > float(level % 8), adj_ref[level], 0.0)
            m_ref[level, lo : lo + 8, :] = level_rows(south_ref, MASK_AT, 4, level, True)
            m_ref[level, hi : hi + 8, :] = level_rows(north_ref, MASK_AT, 4, level, False)
            flow = (zon_ref, mer_ref)[level // 8][0, level % 8]
            f_ref[level, mid : mid + ROWS, :] = 0.5 * flow.astype(jnp.float32)
            f_ref[level, lo : lo + 8, :] = level_rows(south_ref, FLOW_AT, 2, level, True)
            f_ref[level, hi : hi + 8, :] = level_rows(north_ref, FLOW_AT, 2, level, False)
        s_ref[DEP, 0, mid : mid + ROWS, :] = depth
        s_ref[DIA, 0, mid : mid + ROWS, :] = diag_ref[...]
        for field, at in ((DEP, DEPTH_AT), (DIA, DIAG_AT)):
            s_ref[field, 0, lo : lo + 8, :] = level_rows(south_ref, at, 4, 0, True)
            s_ref[field, 0, hi : hi + 8, :] = level_rows(north_ref, at, 4, 0, False)

        def sides(r, carry):
            at = pl.ds(pl.multiple_of(HALO + 8 * r, 8), 8)
            for part in range(3):
                src = pl.ds(pl.multiple_of(part * EXT + 8 * r, 8), 8)
                own = o_ref[src, :]
                pa = pa_ref[src, :]
                pb = pb_ref[src, :]
                east = jnp.where(inner, own, jnp.where(even_lon, pa, pb))
                west = jnp.where(inner, jnp.where(even_lon, pb, pa), own)
                for side, value in ((1, east), (2, west)):
                    if part == 0:
                        sm_ref[side - 1, at, :] = value
                        s_ref[B, side, at, :] = over_groups(coup_lane * value)
                    elif part == 1:
                        sf_ref[side - 1, at, :] = value
                    else:
                        s_ref[DEP, side, at, :] = in_every_group(value, 0)
                        s_ref[DIA, side, at, :] = in_every_group(value, 1)
            total = coup[0] * m_ref[0, at, :]
            for level in range(1, 16):
                total = total + coup[level] * m_ref[level, at, :]
            s_ref[B, 0, at, :] = total
            return carry

        lax.fori_loop(0, CHUNKS, sides, 0)

        def rows_at(r, shift=0):
            start = HALO + 8 * r
            return pl.ds(pl.multiple_of(start, 8) if shift == 0 else start + shift, 8)

        def wrap(main, west, east):
            return roll(jnp.where(inner, west, east), -4)

        def west_east(main, z):
            return roll(jnp.where(lane == LANES - 1, z, main), 1), roll(jnp.where(lane == 0, z, main), -1)

        def star(field, part, r):
            centre = s_ref[field, part, rows_at(r), :]
            south = s_ref[field, part, rows_at(r, -1), :]
            north = s_ref[field, part, rows_at(r, 1), :]
            if part == 0:
                z = wrap(centre, s_ref[field, 2, rows_at(r), :], s_ref[field, 1, rows_at(r), :])
                west, east = west_east(centre, z)
            else:
                west, east = roll(centre, 1), roll(centre, -1)
            return centre, west, east, south, north

        def shifted(field, part, r):
            centre, west, east, south, north = star(field, part, r)
            return s_ref[DIA, part, rows_at(r), :] * centre - (west + east + south + north)

        row = lax.broadcasted_iota(jnp.int32, (8, LANES), 0)

        def on_grid(r, value):
            at = 8 * r + row - HALO
            beyond = ((at < 0) & (lat == 0)) | ((at >= ROWS) & (lat == last))
            return jnp.where(beyond, 0.0, value)

        def images(r, carry):
            for part in range(3):
                s_ref[H, part, rows_at(r), :] = on_grid(r, shifted(B, part, r))
            return carry

        lax.fori_loop(0, CHUNKS, images, 0)

        def apply(coef, centre, west, east, south, north):
            c0, cw, ce, cs, cn = coef
            return c0 * centre + cw * west + ce * east + cs * south + cn * north

        def coefficients(u, w, mins, k):
            dep, dw, de, ds, dn = mins
            cw = jnp.where(dw > k, DIFF - u, 0.0)
            ce = jnp.where(de > k, DIFF + u, 0.0)
            cs = jnp.where(ds > k, DIFF - w, 0.0)
            cn = jnp.where(dn > k, DIFF + w, 0.0)
            c0 = jnp.where(dep > k, 1.0 - ((cw + ce) + (cs + cn)), 0.0)
            return c0, cw, ce, cs, cn

        def depths(part, r):
            dep, dw, de, ds, dn = star(DEP, part, r)
            return dep, jnp.minimum(dep, dw), jnp.minimum(dep, de), jnp.minimum(dep, ds), jnp.minimum(dep, dn)

        def advect(r, carry):
            out_at = pl.ds(pl.multiple_of(8 * r, 8), 8)
            at, below, above = rows_at(r), rows_at(r, -1), rows_at(r, 1)
            mins = depths(0, r)
            bs = star(B, 0, r)
            hs = star(H, 0, r)
            zm = jnp.where(inner, sm_ref[1, at, :], sm_ref[0, at, :])
            us = vs = ws = jnp.zeros((8, LANES), jnp.float32)
            for k in range(8):
                coef = coefficients(f_ref[k, at, :], f_ref[8 + k, at, :], mins, float(k))
                for level in (k, k + 8):
                    centre = m_ref[level, at, :]
                    west, east = west_east(centre, roll(zm, -(8 * level + 4)))
                    value = apply(coef, centre, west, east, m_ref[level, below, :], m_ref[level, above, :])
                    am_ref[level, out_at, :] = value
                    us = us + coup[level] * value
                p = apply(coef, *bs)
                q = apply(coef, *hs)
                pq_ref[k, out_at, :] = p
                pq_ref[8 + k, out_at, :] = q
                vs = vs + square[k] * p
                ws = ws + square[k] * q
            s_ref[U, 0, at, :] = us
            s_ref[V, 0, at, :] = vs
            s_ref[W, 0, at, :] = ws
            kept = []
            for part in (1, 2):
                mins = depths(part, r)
                flow = sf_ref[part - 1, at, :]
                turned = roll(flow, 64)
                u = jnp.where(lane < 64, flow, turned)
                w = jnp.where(lane < 64, turned, flow)
                coef = coefficients(u, w, mins, level_of)
                centre = sm_ref[part - 1, at, :]
                value = apply(
                    coef, centre, roll(centre, 1), roll(centre, -1),
                    sm_ref[part - 1, below, :], sm_ref[part - 1, above, :],
                )
                p = apply(coef, *star(B, part, r))
                q = apply(coef, *star(H, part, r))
                s_ref[U, part, at, :] = over_groups(coup_lane * value)
                s_ref[V, part, at, :] = over_groups(square_lane * p)
                s_ref[W, part, at, :] = over_groups(square_lane * q)
                kept.append((value, p, q))
            for slot in range(3):
                z_out_ref[slot, out_at, :] = jnp.where(inner, kept[1][slot], kept[0][slot])
            return carry

        lax.fori_loop(0, CHUNKS, advect, 0)

        def images_two(r, carry):
            for source, target in ((U, HU), (V, HV), (W, HW)):
                for part in range(3):
                    s_ref[target, part, rows_at(r), :] = on_grid(r, shifted(source, part, r))
            return carry

        lax.fori_loop(0, CHUNKS, images_two, 0)

        def gather(r, sums):
            at = rows_at(r)
            new = []
            b = s_ref[B, 0, at, :]
            h = s_ref[H, 0, at, :]
            new += [b * b, b * h, h * h, h * shifted(H, 0, r)]
            fields = [s_ref[field, 0, at, :] for field in (U, V, W)]
            image = [s_ref[field, 0, at, :] for field in (HU, HV, HW)]
            second = [shifted(field, 0, r) for field in (HU, HV, HW)]
            for left, right in ((fields, fields), (fields, image), (image, image), (image, second)):
                new += [left[i] * right[j] for i, j in PAIRS]
            return tuple(s + n for s, n in zip(sums, new))

        zero = jnp.zeros((8, LANES), jnp.float32)
        sums = lax.fori_loop(1, CHUNKS - 1, gather, (zero,) * NSUMS)
        line = jnp.zeros((1, LANES), jnp.float32)
        for index, value in enumerate(sums):
            total = jnp.sum(jnp.sum(value, axis=1, keepdims=True), axis=0, keepdims=True)
            line = jnp.where(lane[0:1, :] == index, total, line)
        sums_ref[...] = jnp.broadcast_to(line, (devices, LANES))

        def hand_over(r, carry):
            at = rows_at(r)
            out_at = pl.ds(pl.multiple_of(8 * r, 8), 8)
            for slot, field in enumerate((B, H, U, V, W, HU, HV, HW, DEP)):
                f_out_ref[slot, out_at, :] = s_ref[field, 0, at, :]
            for slot, field in enumerate((U, V, W, HU, HV, HW, DEP)):
                z_out_ref[3 + slot, out_at, :] = jnp.where(inner, s_ref[field, 2, at, :], s_ref[field, 1, at, :])
            return carry

        lax.fori_loop(0, CHUNKS, hand_over, 0)

    return kernel


def solve(m0, m1, m2, m3):
    mean = m1 / m0
    theta = mean + SHIFT
    spread = m2 - mean * m1
    ratio = spread / (theta * theta * m0)
    curve = m3 - 2.0 * mean * m2 + mean * mean * m1 + SHIFT * spread
    gamma = curve / spread - ratio * theta
    image_factor = -1.0 / (theta * gamma)
    return 1.0 / theta + (mean / theta + ratio) / gamma, image_factor


def finish_kernel(c_ref, zon_ref, mer_ref, am_ref, pq_ref, f_ref, z_ref, sums_ref, out_ref, sens_ref, m_ref, x_ref):
    lane = lane_iota()
    group = lane // 8
    level_of = (group % 8).astype(jnp.float32)
    coup = [c_ref[level // 8, level % 8] for level in range(16)]
    coup_lane = jnp.zeros((8, LANES), jnp.float32)
    for level in range(16):
        coup_lane = jnp.where(group == level, coup[level], coup_lane)

    line = jnp.sum(sums_ref[...], axis=0, keepdims=True)

    def total(index):
        return jnp.sum(jnp.where(lane[0:1, :] == index, line, 0.0), axis=1, keepdims=True)

    a1, e1 = solve(*[total(i) for i in range(4)])
    y = (None, a1, e1)
    factor = (None, a1 * 2.0, e1 * 2.0, a1 * a1, a1 * e1 * 2.0, e1 * e1)
    moments = []
    for kind in range(4):
        base = 4 + kind * len(PAIRS)
        value = total(base)
        for index in range(1, len(PAIRS)):
            value = value + factor[index] * total(base + index)
        moments.append(value)
    a0, e0 = solve(*moments)
    a1, e1, a0, e0 = [jnp.broadcast_to(v, (8, LANES)) for v in (a1, e1, a0, e0)]
    FB, FH, FU, FV, FW, FHU, FHV, FHW, FDEP = range(9)
    ZAM, ZP, ZQ, ZU, ZV, ZW, ZHU, ZHV, ZHW, ZDEP = range(10)

    def middle(r, carry):
        at = pl.ds(pl.multiple_of(8 * r, 8), 8)
        to = pl.ds(pl.multiple_of(8 * r + HALO, 8), 8)
        b = f_ref[FU, at, :] + a1 * f_ref[FV, at, :] + e1 * f_ref[FW, at, :]
        h = f_ref[FHU, at, :] + a1 * f_ref[FHV, at, :] + e1 * f_ref[FHW, at, :]
        x = a0 * b + e0 * h
        x_ref[at, :] = x + a1 * f_ref[FB, at, :] + e1 * f_ref[FH, at, :]
        dep = f_ref[FDEP, at, :]
        for k in range(8):
            both = a1 * pq_ref[k, at, :] + e1 * pq_ref[8 + k, at, :] + jnp.where(dep > float(k), x, 0.0)
            for level in (k, k + 8):
                m_ref[level, to, :] = am_ref[level, at, :] + coup[level] * both
        return carry

    lax.fori_loop(0, CHUNKS, middle, 0)
    sens_ref[...] = x_ref[HALO : HALO + ROWS, :]

    for k in range(16):
        m_ref[k, 0:8, :] = jnp.zeros((8, LANES), jnp.float32)

    def west_east(main, z):
        return roll(jnp.where(lane == LANES - 1, z, main), 1), roll(jnp.where(lane == 0, z, main), -1)

    def advect(r, carry):
        at = pl.ds(pl.multiple_of(8 * r + HALO, 8), 8)
        out_at = pl.ds(pl.multiple_of(8 * r, 8), 8)
        start = 8 * r + 2 * HALO
        here = pl.ds(pl.multiple_of(start, 8), 8)
        below, above = pl.ds(start - 1, 8), pl.ds(start + 1, 8)
        zb = z_ref[ZU, at, :] + a1 * z_ref[ZV, at, :] + e1 * z_ref[ZW, at, :]
        zh = z_ref[ZHU, at, :] + a1 * z_ref[ZHV, at, :] + e1 * z_ref[ZHW, at, :]
        zx = a0 * zb + e0 * zh
        zd = z_ref[ZDEP, at, :]
        zm = z_ref[ZAM, at, :] + coup_lane * (
            a1 * z_ref[ZP, at, :] + e1 * z_ref[ZQ, at, :] + jnp.where(zd > level_of, zx, 0.0)
        )
        dep = f_ref[FDEP, at, :]
        dw, de = west_east(dep, roll(zd, -4))
        ds = f_ref[FDEP, pl.ds(8 * r + HALO - 1, 8), :]
        dn = f_ref[FDEP, pl.ds(8 * r + HALO + 1, 8), :]
        dw, de, ds, dn = [jnp.minimum(dep, d) for d in (dw, de, ds, dn)]
        for k in range(8):
            u = 0.5 * zon_ref[0, k, out_at, :].astype(jnp.float32)
            w = 0.5 * mer_ref[0, k, out_at, :].astype(jnp.float32)
            cw = jnp.where(dw > float(k), DIFF - u, 0.0)
            ce = jnp.where(de > float(k), DIFF + u, 0.0)
            cs = jnp.where(ds > float(k), DIFF - w, 0.0)
            cn = jnp.where(dn > float(k), DIFF + w, 0.0)
            c0 = 1.0 - ((cw + ce) + (cs + cn))
            for level in (k, k + 8):
                centre = m_ref[level, here, :]
                west, east = west_east(centre, roll(zm, -(8 * level + 4)))
                out_ref[level, out_at, :] = (
                    c0 * centre + cw * west + ce * east + cs * m_ref[level, below, :] + cn * m_ref[level, above, :]
                )
        return carry

    lax.fori_loop(0, ROWS // 8, advect, 0)


def whole(shape):
    return pl.BlockSpec(shape, lambda i: (0,) * len(shape))


def step_flow(step):
    return pl.BlockSpec((1, 8, ROWS, LANES), lambda i: (step, 0, 0, 0))


def on_device_of(lon, lat):
    devices = lon * lat
    f32 = jnp.float32

    def array(*shape):
        return jax.ShapeDtypeStruct(shape, f32)

    smem = pl.BlockSpec(memory_space=pltpu.SMEM)
    params = pltpu.CompilerParams(vmem_limit_bytes=48 * 2**20)
    pairs = {}
    for axis, count in (("lon", lon), ("lat", lat)):
        first = [(i, i ^ 1) for i in range(count)]
        second = [(i, (i - 1) % count if i % 2 == 0 else (i + 1) % count) for i in range(count)]
        pairs[axis] = (first, second)

    def swap(axis, a, b):
        first, second = pairs[axis]
        return lax.ppermute(a, axis, first), lax.ppermute(b, axis, second)

    def on_device(adj_tracer, zonal_flow, meridional_flow, depth, coupling, surface_diag):
        adj = adj_tracer.reshape(16, ROWS, LANES)
        block = [whole((16, ROWS, LANES)), step_flow(1), step_flow(1), whole((ROWS, LANES)), whole((ROWS, LANES))]
        block_args = (adj, zonal_flow, meridional_flow, depth, surface_diag)
        message = whole((MSG_ROWS, LANES))
        msg_a, msg_b = pl.pallas_call(
            row_message_kernel,
            grid=(1,),
            in_specs=block,
            out_specs=[message, message],
            out_shape=[array(MSG_ROWS, LANES)] * 2,
            compiler_params=params,
            name="row_messages",
        )(*block_args)
        recv_a, recv_b = swap("lat", msg_a, msg_b)
        columns = whole((3 * EXT, LANES))
        row_scratch = [pltpu.VMEM((MSG_ROWS, LANES), f32)] * 2
        own = pl.pallas_call(
            make_pack_kernel(lat - 1),
            grid=(1,),
            in_specs=block + [message, message],
            out_specs=columns,
            out_shape=array(3 * EXT, LANES),
            scratch_shapes=row_scratch,
            compiler_params=params,
            name="pack_columns",
        )(*block_args, recv_a, recv_b)
        side_a, side_b = swap("lon", own, own)
        outs = [(16, EXT, LANES), (16, EXT, LANES), (9, EXT, LANES), (10, EXT, LANES), (devices, LANES)]
        am, pq, fields, zs, sums = pl.pallas_call(
            make_fields_kernel(lat - 1, devices),
            grid=(1,),
            in_specs=[smem] + block + [message, message, columns, columns, columns],
            out_specs=[whole(s) for s in outs],
            out_shape=[array(*s) for s in outs],
            scratch_shapes=row_scratch
            + [
                pltpu.VMEM((16, PAD, LANES), f32),
                pltpu.VMEM((16, PAD, LANES), f32),
                pltpu.VMEM((10, 3, PAD, LANES), f32),
                pltpu.VMEM((2, PAD, LANES), f32),
                pltpu.VMEM((2, PAD, LANES), f32),
            ],
            compiler_params=params,
            name="fields",
        )(coupling, *block_args, recv_a, recv_b, own, side_a, side_b)
        everyone = lax.all_to_all(sums, ("lon", "lat"), 0, 0, tiled=True)
        out, sens = pl.pallas_call(
            finish_kernel,
            grid=(1,),
            in_specs=[smem, step_flow(0), step_flow(0)] + [whole(s) for s in outs],
            out_specs=[whole((16, ROWS, LANES)), whole((ROWS, LANES))],
            out_shape=[array(16, ROWS, LANES), array(ROWS, LANES)],
            scratch_shapes=[pltpu.VMEM((16, PAD, LANES), f32), pltpu.VMEM((EXT, LANES), f32)],
            compiler_params=params,
            name="finish",
        )(coupling, zonal_flow, meridional_flow, am, pq, fields, zs, everyone)
        return out.reshape(adj_tracer.shape), sens

    return on_device


def solution(mesh):
    in_specs = (
        P(None, None, "lat", "lon"),
        P(None, None, "lat", "lon"),
        P(None, None, "lat", "lon"),
        P("lat", "lon"),
        P(),
        P("lat", "lon"),
    )
    out_specs = (P(None, None, "lat", "lon"), P("lat", "lon"))
    return jax.shard_map(
        on_device_of(mesh.shape["lon"], mesh.shape["lat"]),
        mesh=mesh, in_specs=in_specs, out_specs=out_specs, check_vma=False,
    )
```

time: 366 us -> 46.6 us (0.13)
  blocking collectives: 239 us -> 10 us
  starting transfers between devices: 43.2 us -> 7.24 us
  local copies, waits for them, and re-layouts: 32.5 us -> 4.46 us
  other arithmetic: 25.3 us -> 0 us
  Pallas kernels: 0 us -> 15.5 us
  between operations: 9 us -> 0.68 us
  waiting for transfers between devices: 14.1 us -> 8.36 us
    psum x6 -> x0, blocking collectives: 239 us -> none  [the longest x4 160 us: global_squares(): return lax.psum(jnp.sum(residual * residual), ('lon', 'lat'))]
    ppermute x24 -> x4, starting transfers between devices: 43.2 us -> 7.24 us  [swap(): return (lax.ppermute(a, axis, first), lax.ppermute(b, axis, second))]
    pallas_call x0 -> x4, Pallas kernels: none -> 15.5 us  [the longest x1 11.8 us: on_device(): pl.pallas_call(make_fields_kernel(lat - 1, devices), grid=(1,), in_specs=...]
    concatenate x8 -> x0, other arithmetic: 14 us -> none  [the longest x4 7.7 us: padded(): jnp.concatenate([lax.ppermute(tail, axis, [(i, (i + 1) % count) for i in...]
    slice x14 -> x0, local copies, waits for them, and re-layouts: 11.6 us -> none  [the longest x10 5.33 us: padded(): lax.slice_in_dim(cells, cells.shape[dim] - width, cells.shape[dim], axis=...]
    all_to_all x0 -> x1, blocking collectives: none -> 10 us  [on_device(): everyone = lax.all_to_all(sums, ('lon', 'lat'), 0, 0, tiled=True)]
    ppermute x4 -> x0, local copies, waits for them, and re-layouts: 9.61 us -> none  [the longest x2 4.82 us: padded(): lax.ppermute(head, axis, [((i + 1) % count, i) for i in range(ends)])]
    unnamed x53 -> x16, local copies, waits for them, and re-layouts: 11.3 us -> 4.46 us
  transfers between devices with their start and end apart: 24 -> 4, of which waited for: 8 -> 2; matrix products, arithmetic and copies ran while one was open for 7% -> 0% of each run, Pallas kernels for 0% -> 0%
where the time goes in v1:
time: 46.6 us; the launch traced here: 46.2 us
  Pallas kernels  15.5 us (33%)
  blocking collectives  10 us (21%)
  waiting for transfers between devices  8.36 us (18%)
  starting transfers between devices  7.24 us (16%)
  local copies, waits for them, and re-layouts  4.46 us (10%)
  between operations  0.68 us (1%)
    pallas_call x1, Pallas kernels, on_device(): pl.pallas_call(make_fields_kernel(lat - 1, devices), grid=(1,), in_specs=...  11.8 us
    all_to_all x1, blocking collectives, on_device(): everyone = lax.all_to_all(sums, ('lon', 'lat'), 0, 0, tiled=True)  10 us
    ppermute x4, waiting for transfers between devices, swap(): return (lax.ppermute(a, axis, first), lax.ppermute(b, axis, second))  8.36 us
    ppermute x4, starting transfers between devices, swap(): return (lax.ppermute(a, axis, first), lax.ppermute(b, axis, second))  7.24 us
    unnamed x16, local copies, waits for them, and re-layouts  4.46 us
    pallas_call x1, Pallas kernels, on_device(): pl.pallas_call(finish_kernel, grid=(1,), in_specs=[smem, step_flow(0), st...  3.16 us
  transfers between devices with their start and end apart: 4, of which 2 were waited for; matrix products, arithmetic and copies ran while one was open for 0% of the time, Pallas kernels for 0%

profile of v1, /device:TPU:0, one launch (start us, length us, event | category | flops | bytes accessed | tf_op | source)
XLA Modules:
  0.0 46.2 jit_solution(15298646380582644515)
XLA Ops:
  0.6 0.0 copy-start
  0.6 1.0 %copy-done = f32[2,8,64,128]{3,2,1,0:T(8,128)S(1)} copy-done((f32[2,8,64,128]{3,2,1,0:T(8,128)S(1)}, f32[2,8,64,128]{3,2,1,0:T(8,128)}, u32[]{:S(2)}) %copy-start) | copy-done | bytes 524312
  1.7 0.0 copy-start.1
  1.7 0.9 %copy-done.1 = bf16[2,8,64,128]{3,2,1,0:T(8,128)(2,1)S(1)} copy-done((bf16[2,8,64,128]{3,2,1,0:T(8,128)(2,1)S(1)}, bf16[2,8,64,128]{3,2,1,0:T(8,128)(2,1)}, u32[]{:S(2)}) %copy-start.1) | copy-done | bytes 262168
  2.6 0.9 %copy-done.3 = bf16[2,8,64,128]{3,2,1,0:T(8,128)(2,1)S(1)} copy-done((bf16[2,8,64,128]{3,2,1,0:T(8,128)(2,1)S(1)}, bf16[2,8,64,128]{3,2,1,0:T(8,128)(2,1)}, u32[]{:S(2)}) %copy-start.3) | copy-done | bytes 262168
  3.6 0.8 %copy-done.5 = s32[64,128]{1,0:T(8,128)S(1)} copy-done((s32[64,128]{1,0:T(8,128)S(1)}, s32[64,128]{1,0:T(8,128)}, u32[]{:S(2)}) %copy-start.5) | copy-done | bytes 32792
  4.3 0.8 %copy-done.6 = f32[64,128]{1,0:T(8,128)S(1)} copy-done((f32[64,128]{1,0:T(8,128)S(1)}, f32[64,128]{1,0:T(8,128)}, u32[]{:S(2)}) %copy-start.6) | copy-done | bytes 32792
  5.1 3.1 %collective-permute-start = (f32[120,128]{1,0:T(8,128)S(1)}, f32[120,128]{1,0:T(8,128)S(1)}, u32[]{:S(2)}, u32[]{:S(2)}) collective-permute-start(f32[120,128]{1,0:T(8,128)S(1)} %get-tuple-element.11), channel_id=1, source_target_pairs={{0,1},{1,0},{2,3},{3,2},{4,5},{5,4},{6,7},{7,6},{8,9},{9,8},{10,11... | collective-permute-start | bytes 184328 | tf_op jit(solution)/shard_map/ppermute | solution.py:469
  8.2 2.5 %collective-permute-start.1 = (f32[120,128]{1,0:T(8,128)S(1)}, f32[120,128]{1,0:T(8,128)S(1)}, u32[]{:S(2)}, u32[]{:S(2)}) collective-permute-start(f32[120,128]{1,0:T(8,128)S(1)} %get-tuple-element.12), channel_id=1, source_target_pairs={{0,3},{1,2},{2,1},{3,0},{4,7},{5,6},{6,5},{7,4},{8,11},{9,10},{10,... | collective-permute-start | bytes 184328 | tf_op jit(solution)/shard_map/ppermute | solution.py:469
  10.7 0.0 collective-permute-done.ra_ref
  10.7 3.5 %collective-permute-done.1.rb_ref = f32[120,128]{1,0:T(8,128)S(1)} collective-permute-done((f32[120,128]{1,0:T(8,128)S(1)}, f32[120,128]{1,0:T(8,128)S(1)}, u32[]{:S(2)}, u32[]{:S(2)}) %collective-permute-start.1) | collective-permute-done | bytes 61472 | tf_op jit(solution)/shard_map/ppermute | solution.py:469
  14.2 0.4 pack_columns.1.o_ref
  14.7 0.0 copy-start.2
  14.7 0.0 copy-start.4
  14.7 1.1 %collective-permute-start.3 = (f32[240,128]{1,0:T(8,128)S(1)}, f32[240,128]{1,0:T(8,128)S(1)}, u32[]{:S(2)}, u32[]{:S(2)}) collective-permute-start(f32[240,128]{1,0:T(8,128)S(1)} %pack_columns.1.o_ref), channel_id=1, source_target_pairs={{0,28},{4,8},{8,4},{12,16},{16,12},{20,24},{24,20},{28,0},{1,29},{... | collective-permute-start | bytes 368648 | tf_op jit(solution)/shard_map/ppermute | solution.py:469
  15.8 0.6 %collective-permute-start.2 = (f32[240,128]{1,0:T(8,128)S(1)}, f32[240,128]{1,0:T(8,128)S(1)}, u32[]{:S(2)}, u32[]{:S(2)}) collective-permute-start(f32[240,128]{1,0:T(8,128)S(1)} %pack_columns.1.o_ref), channel_id=1, source_target_pairs={{0,4},{4,0},{8,12},{12,8},{16,20},{20,16},{24,28},{28,24},{1,5},{5... | collective-permute-start | bytes 368648 | tf_op jit(solution)/shard_map/ppermute | solution.py:469
  16.4 4.8 %collective-permute-done.3.pb_ref = f32[240,128]{1,0:T(8,128)S(1)} collective-permute-done((f32[240,128]{1,0:T(8,128)S(1)}, f32[240,128]{1,0:T(8,128)S(1)}, u32[]{:S(2)}, u32[]{:S(2)}) %collective-permute-start.3) | collective-permute-done | bytes 122912 | tf_op jit(solution)/shard_map/ppermute | solution.py:469
  21.2 0.0 collective-permute-done.2.pa_ref
  21.2 0.0 copy-done.7
  21.2 11.8 %fields.1 = (f32[16,80,128]{2,1,0:T(8,128)S(1)}, f32[16,80,128]{2,1,0:T(8,128)S(1)}, f32[9,80,128]{2,1,0:T(8,128)S(1)}, f32[10,80,128]{2,1,0:T(8,128)S(1)}, f32[32,128]{1,0:T(8,128)S(1)}) custom-call(f32[2,8]{1,0:T(2,128)S(1)} %copy-done.7, f32[16,64,128]{2,1,0:T(8,128)S(1)} %bitcast.8, bf16[2,8,64,128]{3,2,1,0:T(8,128)(2,1)S(1)} %copy-done.1, ...), custom_call_target="tpu_custom_call" | custom-call | tf_op jit(solution)/shard_map/fields/pallas_call | solution.py:500
  33.0 10.0 %all_to_all.11 = f32[32,1,128]{2,1,0:T(1,128)S(1)} all-to-all(f32[32,1,128]{2,1,0:T(1,128)S(1)} %bitcast.10), channel_id=1, replica_groups=mesh['lon'=8,'lat'=4] {'lon','lat'}, dimensions={0} | all-to-all | bytes 32768 | tf_op jit(solution)/shard_map/all_to_all | solution.py:517
  43.0 0.0 copy-done.2
  43.0 0.0 copy-done.4
  43.0 3.2 %finish.1 = (f32[16,64,128]{2,1,0:T(8,128)}, f32[64,128]{1,0:T(8,128)}) custom-call(f32[2,8]{1,0:T(2,128)S(1)} %copy-done.7, bf16[2,8,64,128]{3,2,1,0:T(8,128)(2,1)S(1)} %copy-done.2, bf16[2,8,64,128]{3,2,1,0:T(8,128)(2,1)S(1)} %copy-done.4, f32[16,80,128]{2,1,0:T(8,128)S(1)} %get-tuple-element.13.am_ref, f32[16,80,128]{2,1,0:T(8,128)S(1)} %get-tuple-element.14.pq_ref, ...), custom_call_target="tpu_custom_call" | custom-call | tf_op jit(solution)/shard_map/finish/pallas_call | solution.py:518
  (5 shorter events, 0.0 us)
Async XLA Ops:
  0.6 1.0 %copy-start = (f32[2,8,64,128]{3,2,1,0:T(8,128)S(1)}, f32[2,8,64,128]{3,2,1,0:T(8,128)}, u32[]{:S(2)}) copy-start(f32[2,8,64,128]{3,2,1,0:T(8,128)} %param.6) | copy-start | bytes 1572868
  1.7 0.9 %copy-start.1 = (bf16[2,8,64,128]{3,2,1,0:T(8,128)(2,1)S(1)}, bf16[2,8,64,128]{3,2,1,0:T(8,128)(2,1)}, u32[]{:S(2)}) copy-start(bf16[2,8,64,128]{3,2,1,0:T(8,128)(2,1)} %zon_ref.5) | copy-start | bytes 786436
  2.6 0.9 %copy-start.3 = (bf16[2,8,64,128]{3,2,1,0:T(8,128)(2,1)S(1)}, bf16[2,8,64,128]{3,2,1,0:T(8,128)(2,1)}, u32[]{:S(2)}) copy-start(bf16[2,8,64,128]{3,2,1,0:T(8,128)(2,1)} %mer_ref.5) | copy-start | bytes 786436
  3.6 0.8 %copy-start.5 = (s32[64,128]{1,0:T(8,128)S(1)}, s32[64,128]{1,0:T(8,128)}, u32[]{:S(2)}) copy-start(s32[64,128]{1,0:T(8,128)} %depth_ref.3) | copy-start | bytes 98308
  4.3 0.8 %copy-start.6 = (f32[64,128]{1,0:T(8,128)S(1)}, f32[64,128]{1,0:T(8,128)}, u32[]{:S(2)}) copy-start(f32[64,128]{1,0:T(8,128)} %diag_ref.3) | copy-start | bytes 98308
  5.1 5.6 %collective-permute-start = (f32[120,128]{1,0:T(8,128)S(1)}, f32[120,128]{1,0:T(8,128)S(1)}, u32[]{:S(2)}, u32[]{:S(2)}) collective-permute-start(f32[120,128]{1,0:T(8,128)S(1)} %get-tuple-element.11), channel_id=1, source_target_pairs={{0,1},{1,0},{2,3},{3,2},{4,5},{5,4},{6,7},{7,6},{8,9},{9,8},{10,11... | collective-permute-start | bytes 184328 | tf_op jit(solution)/shard_map/ppermute | solution.py:469
  8.2 13.0 %copy-start.7 = (f32[2,8]{1,0:T(2,128)S(1)}, f32[2,8]{1,0:T(2,128)}, u32[]{:S(2)}) copy-start(f32[2,8]{1,0:T(2,128)} %c_ref.3) | copy-start | bytes 196
  8.2 6.0 %collective-permute-start.1 = (f32[120,128]{1,0:T(8,128)S(1)}, f32[120,128]{1,0:T(8,128)S(1)}, u32[]{:S(2)}, u32[]{:S(2)}) collective-permute-start(f32[120,128]{1,0:T(8,128)S(1)} %get-tuple-element.12), channel_id=1, source_target_pairs={{0,3},{1,2},{2,1},{3,0},{4,7},{5,6},{6,5},{7,4},{8,11},{9,10},{10,... | collective-permute-start | bytes 184328 | tf_op jit(solution)/shard_map/ppermute | solution.py:469
  14.7 28.4 %copy-start.2 = (bf16[2,8,64,128]{3,2,1,0:T(8,128)(2,1)S(1)}, bf16[2,8,64,128]{3,2,1,0:T(8,128)(2,1)}, u32[]{:S(2)}) copy-start(bf16[2,8,64,128]{3,2,1,0:T(8,128)(2,1)} %zon_ref.5) | copy-start | bytes 786436
  14.7 28.4 %copy-start.4 = (bf16[2,8,64,128]{3,2,1,0:T(8,128)(2,1)S(1)}, bf16[2,8,64,128]{3,2,1,0:T(8,128)(2,1)}, u32[]{:S(2)}) copy-start(bf16[2,8,64,128]{3,2,1,0:T(8,128)(2,1)} %mer_ref.5) | copy-start | bytes 786436
  14.7 6.5 %collective-permute-start.3 = (f32[240,128]{1,0:T(8,128)S(1)}, f32[240,128]{1,0:T(8,128)S(1)}, u32[]{:S(2)}, u32[]{:S(2)}) collective-permute-start(f32[240,128]{1,0:T(8,128)S(1)} %pack_columns.1.o_ref), channel_id=1, source_target_pairs={{0,28},{4,8},{8,4},{12,16},{16,12},{20,24},{24,20},{28,0},{1,29},{... | collective-permute-start | bytes 368648 | tf_op jit(solution)/shard_map/ppermute | solution.py:469
  15.8 5.4 %collective-permute-start.2 = (f32[240,128]{1,0:T(8,128)S(1)}, f32[240,128]{1,0:T(8,128)S(1)}, u32[]{:S(2)}, u32[]{:S(2)}) collective-permute-start(f32[240,128]{1,0:T(8,128)S(1)} %pack_columns.1.o_ref), channel_id=1, source_target_pairs={{0,4},{4,0},{8,12},{12,8},{16,20},{20,16},{24,28},{28,24},{1,5},{5... | collective-permute-start | bytes 368648 | tf_op jit(solution)/shard_map/ppermute | solution.py:469

commit v2 on v1

--- a/solution.py
+++ b/solution.py
@@ -44,37 +44,45 @@
     return ref[pl.ds(start - (8 - count) if south else start, 8), :]
 
 
-def row_messages(coupling_free_refs):
-    adj_ref, zon_ref, mer_ref, depth_ref, diag_ref, a_ref, b_ref = coupling_free_refs
+def row_message_kernel(adj, zon, mer, depth, diag, a_ref, b_ref, adj_ref, flow_ref, depth_ref, diag_ref, sems):
+    copies = []
+    for edge, start in ((0, 0), (1, ROWS - 8)):
+        rows = pl.ds(start, 8)
+        for source, target in (
+            (adj.at[:, rows, :], adj_ref.at[edge]),
+            (zon.at[1, :, rows, :], flow_ref.at[edge, 0]),
+            (mer.at[1, :, rows, :], flow_ref.at[edge, 1]),
+            (depth.at[rows, :], depth_ref.at[edge]),
+            (diag.at[rows, :], diag_ref.at[edge]),
+        ):
+            copies.append(pltpu.make_async_copy(source, target, sems.at[len(copies)]))
+            copies[-1].start()
     even = lax.rem(lax.axis_index("lat"), 2) == 0
     zero = jnp.zeros((8, LANES), jnp.float32)
     for ref in (a_ref, b_ref):
         ref[0:8, :] = zero
         ref[MSG_ROWS - 8 : MSG_ROWS, :] = zero
+    for copy in copies:
+        copy.wait()
 
     def put(at, low, high):
         count = low.shape[0]
         a_ref[pl.ds(at, count), :] = jnp.where(even, high, low)
         b_ref[pl.ds(at, count), :] = jnp.where(even, low, high)
 
-    depth_low = depth_ref[0:4, :].astype(jnp.float32)
-    depth_high = depth_ref[ROWS - 4 : ROWS, :].astype(jnp.float32)
+    depth_low = depth_ref[0, 0:4, :].astype(jnp.float32)
+    depth_high = depth_ref[1, 4:8, :].astype(jnp.float32)
     for level in range(16):
         k = float(level % 8)
-        low = jnp.where(depth_low > k, adj_ref[level, 0:4, :], 0.0)
-        high = jnp.where(depth_high > k, adj_ref[level, ROWS - 4 : ROWS, :], 0.0)
+        low = jnp.where(depth_low > k, adj_ref[0, level, 0:4, :], 0.0)
+        high = jnp.where(depth_high > k, adj_ref[1, level, 4:8, :], 0.0)
         put(MASK_AT + 4 * level, low, high)
     put(DEPTH_AT, depth_low, depth_high)
-    put(DIAG_AT, diag_ref[0:4, :], diag_ref[ROWS - 4 : ROWS, :])
-    for which, ref in enumerate((zon_ref, mer_ref)):
-        for k in range(8):
-            low = 0.5 * ref[0, k, 0:16, :].astype(jnp.float32)
-            high = 0.5 * ref[0, k, ROWS - 16 : ROWS, :].astype(jnp.float32)
-            put(FLOW_AT + 2 * (8 * which + k), low[0:2], high[14:16])
-
-
-def row_message_kernel(*refs):
-    row_messages(refs)
+    put(DIAG_AT, diag_ref[0, 0:4, :], diag_ref[1, 4:8, :])
+    for level in range(16):
+        low = 0.5 * flow_ref[0, level // 8, level % 8].astype(jnp.float32)
+        high = 0.5 * flow_ref[1, level // 8, level % 8].astype(jnp.float32)
+        put(FLOW_AT + 2 * level, low[0:2], high[6:8])
 
 
 def sort_rows(recv_a_ref, recv_b_ref, south_ref, north_ref, last):
@@ -104,7 +112,7 @@
         for which, ref in enumerate((zon_ref, mer_ref)):
             for k in range(8):
                 level = 8 * which + k
-                value = 0.5 * ref[0, k].astype(jnp.float32)
+                value = 0.5 * ref[1, k].astype(jnp.float32)
                 packed = jnp.where(group == level, roll(value, 8 * level + 4), packed)
         o_ref[EXT + HALO : EXT + HALO + ROWS, :] = packed
         packed = jnp.where(group == 0, roll(depth, 4), roll(diag_ref[...], 12))
@@ -156,7 +164,7 @@
             m_ref[level, mid : mid + ROWS, :] = jnp.where(depth > float(level % 8), adj_ref[level], 0.0)
             m_ref[level, lo : lo + 8, :] = level_rows(south_ref, MASK_AT, 4, level, True)
             m_ref[level, hi : hi + 8, :] = level_rows(north_ref, MASK_AT, 4, level, False)
-            flow = (zon_ref, mer_ref)[level // 8][0, level % 8]
+            flow = (zon_ref, mer_ref)[level // 8][1, level % 8]
             f_ref[level, mid : mid + ROWS, :] = 0.5 * flow.astype(jnp.float32)
             f_ref[level, lo : lo + 8, :] = level_rows(south_ref, FLOW_AT, 2, level, True)
             f_ref[level, hi : hi + 8, :] = level_rows(north_ref, FLOW_AT, 2, level, False)
@@ -190,7 +198,7 @@
             s_ref[B, 0, at, :] = total
             return carry
 
-        lax.fori_loop(0, CHUNKS, sides, 0)
+        lax.fori_loop(0, CHUNKS, sides, 0, unroll=True)
 
         def rows_at(r, shift=0):
             start = HALO + 8 * r
@@ -229,7 +237,7 @@
                 s_ref[H, part, rows_at(r), :] = on_grid(r, shifted(B, part, r))
             return carry
 
-        lax.fori_loop(0, CHUNKS, images, 0)
+        lax.fori_loop(0, CHUNKS, images, 0, unroll=True)
 
         def apply(coef, centre, west, east, south, north):
             c0, cw, ce, cs, cn = coef
@@ -304,7 +312,7 @@
                     s_ref[target, part, rows_at(r), :] = on_grid(r, shifted(source, part, r))
             return carry
 
-        lax.fori_loop(0, CHUNKS, images_two, 0)
+        lax.fori_loop(0, CHUNKS, images_two, 0, unroll=True)
 
         def gather(r, sums):
             at = rows_at(r)
@@ -320,7 +328,7 @@
             return tuple(s + n for s, n in zip(sums, new))
 
         zero = jnp.zeros((8, LANES), jnp.float32)
-        sums = lax.fori_loop(1, CHUNKS - 1, gather, (zero,) * NSUMS)
+        sums = lax.fori_loop(1, CHUNKS - 1, gather, (zero,) * NSUMS, unroll=True)
         line = jnp.zeros((1, LANES), jnp.float32)
         for index, value in enumerate(sums):
             total = jnp.sum(jnp.sum(value, axis=1, keepdims=True), axis=0, keepdims=True)
@@ -336,7 +344,7 @@
                 z_out_ref[3 + slot, out_at, :] = jnp.where(inner, s_ref[field, 2, at, :], s_ref[field, 1, at, :])
             return carry
 
-        lax.fori_loop(0, CHUNKS, hand_over, 0)
+        lax.fori_loop(0, CHUNKS, hand_over, 0, unroll=True)
 
     return kernel
 
@@ -395,7 +403,7 @@
                 m_ref[level, to, :] = am_ref[level, at, :] + coup[level] * both
         return carry
 
-    lax.fori_loop(0, CHUNKS, middle, 0)
+    lax.fori_loop(0, CHUNKS, middle, 0, unroll=2)
     sens_ref[...] = x_ref[HALO : HALO + ROWS, :]
 
     for k in range(16):
@@ -438,15 +446,11 @@
                 )
         return carry
 
-    lax.fori_loop(0, ROWS // 8, advect, 0)
-
-
-def whole(shape):
-    return pl.BlockSpec(shape, lambda i: (0,) * len(shape))
-
-
-def step_flow(step):
-    return pl.BlockSpec((1, 8, ROWS, LANES), lambda i: (step, 0, 0, 0))
+    lax.fori_loop(0, ROWS // 8, advect, 0, unroll=2)
+
+
+VMEM = pl.BlockSpec(memory_space=pltpu.VMEM)
+HBM = pl.BlockSpec(memory_space=pltpu.HBM)
 
 
 def on_device_of(lon, lat):
@@ -470,26 +474,28 @@
 
     def on_device(adj_tracer, zonal_flow, meridional_flow, depth, coupling, surface_diag):
         adj = adj_tracer.reshape(16, ROWS, LANES)
-        block = [whole((16, ROWS, LANES)), step_flow(1), step_flow(1), whole((ROWS, LANES)), whole((ROWS, LANES))]
         block_args = (adj, zonal_flow, meridional_flow, depth, surface_diag)
-        message = whole((MSG_ROWS, LANES))
         msg_a, msg_b = pl.pallas_call(
             row_message_kernel,
-            grid=(1,),
-            in_specs=block,
-            out_specs=[message, message],
+            in_specs=[HBM] * 5,
+            out_specs=[VMEM] * 2,
             out_shape=[array(MSG_ROWS, LANES)] * 2,
-            compiler_params=params,
+            scratch_shapes=[
+                pltpu.VMEM((2, 16, 8, LANES), f32),
+                pltpu.VMEM((2, 2, 8, 8, LANES), jnp.bfloat16),
+                pltpu.VMEM((2, 8, LANES), jnp.int32),
+                pltpu.VMEM((2, 8, LANES), f32),
+                pltpu.SemaphoreType.DMA((10,)),
+            ],
+            compiler_params=pltpu.CompilerParams(vmem_limit_bytes=62914560),
             name="row_messages",
         )(*block_args)
         recv_a, recv_b = swap("lat", msg_a, msg_b)
-        columns = whole((3 * EXT, LANES))
         row_scratch = [pltpu.VMEM((MSG_ROWS, LANES), f32)] * 2
         own = pl.pallas_call(
             make_pack_kernel(lat - 1),
-            grid=(1,),
-            in_specs=block + [message, message],
-            out_specs=columns,
+            in_specs=[VMEM] * 7,
+            out_specs=VMEM,
             out_shape=array(3 * EXT, LANES),
             scratch_shapes=row_scratch,
             compiler_params=params,
@@ -499,9 +505,8 @@
         outs = [(16, EXT, LANES), (16, EXT, LANES), (9, EXT, LANES), (10, EXT, LANES), (devices, LANES)]
         am, pq, fields, zs, sums = pl.pallas_call(
             make_fields_kernel(lat - 1, devices),
-            grid=(1,),
-            in_specs=[smem] + block + [message, message, columns, columns, columns],
-            out_specs=[whole(s) for s in outs],
+            in_specs=[smem] + [VMEM] * 10,
+            out_specs=[VMEM] * 5,
             out_shape=[array(*s) for s in outs],
             scratch_shapes=row_scratch
             + [
@@ -517,9 +522,8 @@
         everyone = lax.all_to_all(sums, ("lon", "lat"), 0, 0, tiled=True)
         out, sens = pl.pallas_call(
             finish_kernel,
-            grid=(1,),
-            in_specs=[smem, step_flow(0), step_flow(0)] + [whole(s) for s in outs],
-            out_specs=[whole((16, ROWS, LANES)), whole((ROWS, LANES))],
+            in_specs=[smem] + [VMEM] * 7,
+            out_specs=[VMEM] * 2,
             out_shape=[array(16, ROWS, LANES), array(ROWS, LANES)],
             scratch_shapes=[pltpu.VMEM((16, PAD, LANES), f32), pltpu.VMEM((EXT, LANES), f32)],
             compiler_params=params,

time: 46.6 us -> 39.4 us (0.85)
  local copies, waits for them, and re-layouts: 4.46 us -> 0.02 us
  Pallas kernels: 15.5 us -> 12.7 us
    unnamed x16 -> x12, local copies, waits for them, and re-layouts: 4.46 us -> 0.02 us
    pallas_call x4, Pallas kernels: 15.5 us -> 12.7 us  [the longest x1 7.95 us: on_device(): pl.pallas_call(make_fields_kernel(lat - 1, devices), in_specs=[smem] + [V...]
where the time goes in v2:
time: 39.4 us; the launch traced here: 39.2 us
  Pallas kernels  12.7 us (32%)
  blocking collectives  10 us (25%)
  waiting for transfers between devices  8.57 us (22%)
  starting transfers between devices  7.24 us (18%)
  between operations  0.72 us (2%)
    all_to_all x1, blocking collectives, on_device(): everyone = lax.all_to_all(sums, ('lon', 'lat'), 0, 0, tiled=True)  10 us
    ppermute x4, waiting for transfers between devices, swap(): return (lax.ppermute(a, axis, first), lax.ppermute(b, axis, second))  8.57 us
    pallas_call x1, Pallas kernels, on_device(): pl.pallas_call(make_fields_kernel(lat - 1, devices), in_specs=[smem] + [V...  7.95 us
    ppermute x4, starting transfers between devices, swap(): return (lax.ppermute(a, axis, first), lax.ppermute(b, axis, second))  7.24 us
    pallas_call x1, Pallas kernels, on_device(): pl.pallas_call(finish_kernel, in_specs=[smem] + [VMEM] * 7, out_specs=[VM...  2.56 us
    pallas_call x1, Pallas kernels, on_device(): pl.pallas_call(row_message_kernel, in_specs=[HBM] * 5, out_specs=[VMEM] *...  1.77 us
  transfers between devices with their start and end apart: 4, of which 2 were waited for; matrix products, arithmetic and copies ran while one was open for 0% of the time, Pallas kernels for 0%

profile of v2, /device:TPU:0, one launch (start us, length us, event | category | flops | bytes accessed | tf_op | source)
XLA Modules:
  0.0 39.2 jit_solution(13954420557018696696)
XLA Ops:
  0.6 0.0 copy-start
  0.6 0.0 copy-start.1
  0.7 0.0 copy-start.2
  0.7 0.0 copy-start.3
  0.7 0.0 copy-start.4
  0.7 1.8 %row_messages.1 = (f32[120,128]{1,0:T(8,128)}, f32[120,128]{1,0:T(8,128)}) custom-call(f32[16,64,128]{2,1,0:T(8,128)} %bitcast.6, bf16[2,8,64,128]{3,2,1,0:T(8,128)(2,1)} %zon_ref.5, bf16[2,8,64,128]{3,2,1,0:T(8,128)(2,1)} %mer_ref.5, s32[64,128]{1,0:T(8,128)} %depth_ref.3, f32[64,128]{1,0:T(8,128)} %diag_ref.3), custom_call_target="tpu_custom_call" | custom-call | tf_op jit(solution)/shard_map/row_messages/pallas_call | solution.py:478
  2.5 3.1 %collective-permute-start = (f32[120,128]{1,0:T(8,128)}, f32[120,128]{1,0:T(8,128)S(1)}, u32[]{:S(2)}, u32[]{:S(2)}) collective-permute-start(f32[120,128]{1,0:T(8,128)} %get-tuple-element.11), channel_id=1, source_target_pairs={{0,1},{1,0},{2,3},{3,2},{4,5},{5,4},{6,7},{7,6},{8,9},{9,8},{10,11... | collective-permute-start | bytes 184328 | tf_op jit(solution)/shard_map/ppermute | solution.py:473
  5.6 2.5 %collective-permute-start.1 = (f32[120,128]{1,0:T(8,128)}, f32[120,128]{1,0:T(8,128)S(1)}, u32[]{:S(2)}, u32[]{:S(2)}) collective-permute-start(f32[120,128]{1,0:T(8,128)} %get-tuple-element.12), channel_id=1, source_target_pairs={{0,3},{1,2},{2,1},{3,0},{4,7},{5,6},{6,5},{7,4},{8,11},{9,10},{10,... | collective-permute-start | bytes 184328 | tf_op jit(solution)/shard_map/ppermute | solution.py:473
  8.0 0.0 collective-permute-done.ra_ref
  8.0 3.8 %collective-permute-done.1.rb_ref = f32[120,128]{1,0:T(8,128)S(1)} collective-permute-done((f32[120,128]{1,0:T(8,128)}, f32[120,128]{1,0:T(8,128)S(1)}, u32[]{:S(2)}, u32[]{:S(2)}) %collective-permute-start.1) | collective-permute-done | bytes 61472 | tf_op jit(solution)/shard_map/ppermute | solution.py:473
  11.8 0.0 copy-done
  11.8 0.0 copy-done.1
  11.8 0.0 copy-done.2
  11.8 0.0 copy-done.3
  11.8 0.0 copy-done.4
  11.8 0.4 %pack_columns.1.o_ref = f32[240,128]{1,0:T(8,128)S(1)} custom-call(f32[16,64,128]{2,1,0:T(8,128)S(1)} %bitcast.7, bf16[2,8,64,128]{3,2,1,0:T(8,128)(2,1)S(1)} %copy-done.1, bf16[2,8,64,128]{3,2,1,0:T(8,128)(2,1)S(1)} %copy-done.2, s32[64,128]{1,0:T(8,128)S(1)} %copy-done.3, f32[64,128]{1,0:T(8,128)S(1)} %copy-done.4, ...), custom_call_target="tpu_custom_call" | custom-call | tf_op jit(solution)/shard_map/pack_columns/pallas_call | solution.py:495
  12.2 1.1 %collective-permute-start.3 = (f32[240,128]{1,0:T(8,128)S(1)}, f32[240,128]{1,0:T(8,128)S(1)}, u32[]{:S(2)}, u32[]{:S(2)}) collective-permute-start(f32[240,128]{1,0:T(8,128)S(1)} %pack_columns.1.o_ref), channel_id=1, source_target_pairs={{0,28},{4,8},{8,4},{12,16},{16,12},{20,24},{24,20},{28,0},{1,29},{... | collective-permute-start | bytes 368648 | tf_op jit(solution)/shard_map/ppermute | solution.py:473
  13.4 0.6 %collective-permute-start.2 = (f32[240,128]{1,0:T(8,128)S(1)}, f32[240,128]{1,0:T(8,128)S(1)}, u32[]{:S(2)}, u32[]{:S(2)}) collective-permute-start(f32[240,128]{1,0:T(8,128)S(1)} %pack_columns.1.o_ref), channel_id=1, source_target_pairs={{0,4},{4,0},{8,12},{12,8},{16,20},{20,16},{24,28},{28,24},{1,5},{5... | collective-permute-start | bytes 368648 | tf_op jit(solution)/shard_map/ppermute | solution.py:473
  13.9 4.8 %collective-permute-done.3.pb_ref = f32[240,128]{1,0:T(8,128)S(1)} collective-permute-done((f32[240,128]{1,0:T(8,128)S(1)}, f32[240,128]{1,0:T(8,128)S(1)}, u32[]{:S(2)}, u32[]{:S(2)}) %collective-permute-start.3) | collective-permute-done | bytes 122912 | tf_op jit(solution)/shard_map/ppermute | solution.py:473
  18.7 0.0 collective-permute-done.2.pa_ref
  18.7 0.0 copy-done.5
  18.7 7.9 %fields.1 = (f32[16,80,128]{2,1,0:T(8,128)S(1)}, f32[16,80,128]{2,1,0:T(8,128)S(1)}, f32[9,80,128]{2,1,0:T(8,128)S(1)}, f32[10,80,128]{2,1,0:T(8,128)S(1)}, f32[32,128]{1,0:T(8,128)S(1)}) custom-call(f32[2,8]{1,0:T(2,128)S(1)} %copy-done.5, f32[16,64,128]{2,1,0:T(8,128)S(1)} %bitcast.8, bf16[2,8,64,128]{3,2,1,0:T(8,128)(2,1)S(1)} %copy-done.1, ...), custom_call_target="tpu_custom_call" | custom-call | tf_op jit(solution)/shard_map/fields/pallas_call | solution.py:506
  26.7 10.0 %all_to_all.11 = f32[32,1,128]{2,1,0:T(1,128)S(1)} all-to-all(f32[32,1,128]{2,1,0:T(1,128)S(1)} %bitcast.10), channel_id=1, replica_groups=mesh['lon'=8,'lat'=4] {'lon','lat'}, dimensions={0} | all-to-all | bytes 32768 | tf_op jit(solution)/shard_map/all_to_all | solution.py:522
  36.7 2.6 %finish.1 = (f32[16,64,128]{2,1,0:T(8,128)}, f32[64,128]{1,0:T(8,128)}) custom-call(f32[2,8]{1,0:T(2,128)S(1)} %copy-done.5, bf16[2,8,64,128]{3,2,1,0:T(8,128)(2,1)S(1)} %copy-done.1, bf16[2,8,64,128]{3,2,1,0:T(8,128)(2,1)S(1)} %copy-done.2, f32[16,80,128]{2,1,0:T(8,128)S(1)} %get-tuple-element.13.am_ref, f32[16,80,128]{2,1,0:T(8,128)S(1)} %get-tuple-element.14.pq_ref, ...), custom_call_target="tpu_custom_call" | custom-call | tf_op jit(solution)/shard_map/finish/pallas_call | solution.py:523
  (1 shorter events, 0.0 us)
Async XLA Ops:
  0.6 11.2 %copy-start = (f32[2,8,64,128]{3,2,1,0:T(8,128)S(1)}, f32[2,8,64,128]{3,2,1,0:T(8,128)}, u32[]{:S(2)}) copy-start(f32[2,8,64,128]{3,2,1,0:T(8,128)} %param.6) | copy-start | bytes 1572868
  0.6 11.1 %copy-start.1 = (bf16[2,8,64,128]{3,2,1,0:T(8,128)(2,1)S(1)}, bf16[2,8,64,128]{3,2,1,0:T(8,128)(2,1)}, u32[]{:S(2)}) copy-start(bf16[2,8,64,128]{3,2,1,0:T(8,128)(2,1)} %zon_ref.5) | copy-start | bytes 786436
  0.7 11.1 %copy-start.2 = (bf16[2,8,64,128]{3,2,1,0:T(8,128)(2,1)S(1)}, bf16[2,8,64,128]{3,2,1,0:T(8,128)(2,1)}, u32[]{:S(2)}) copy-start(bf16[2,8,64,128]{3,2,1,0:T(8,128)(2,1)} %mer_ref.5) | copy-start | bytes 786436
  0.7 11.1 %copy-start.3 = (s32[64,128]{1,0:T(8,128)S(1)}, s32[64,128]{1,0:T(8,128)}, u32[]{:S(2)}) copy-start(s32[64,128]{1,0:T(8,128)} %depth_ref.3) | copy-start | bytes 98308
  0.7 11.1 %copy-start.4 = (f32[64,128]{1,0:T(8,128)S(1)}, f32[64,128]{1,0:T(8,128)}, u32[]{:S(2)}) copy-start(f32[64,128]{1,0:T(8,128)} %diag_ref.3) | copy-start | bytes 98308
  2.5 5.6 %collective-permute-start = (f32[120,128]{1,0:T(8,128)}, f32[120,128]{1,0:T(8,128)S(1)}, u32[]{:S(2)}, u32[]{:S(2)}) collective-permute-start(f32[120,128]{1,0:T(8,128)} %get-tuple-element.11), channel_id=1, source_target_pairs={{0,1},{1,0},{2,3},{3,2},{4,5},{5,4},{6,7},{7,6},{8,9},{9,8},{10,11... | collective-permute-start | bytes 184328 | tf_op jit(solution)/shard_map/ppermute | solution.py:473
  5.6 13.2 %copy-start.5 = (f32[2,8]{1,0:T(2,128)S(1)}, f32[2,8]{1,0:T(2,128)}, u32[]{:S(2)}) copy-start(f32[2,8]{1,0:T(2,128)} %c_ref.3) | copy-start | bytes 196
  5.6 6.2 %collective-permute-start.1 = (f32[120,128]{1,0:T(8,128)}, f32[120,128]{1,0:T(8,128)S(1)}, u32[]{:S(2)}, u32[]{:S(2)}) collective-permute-start(f32[120,128]{1,0:T(8,128)} %get-tuple-element.12), channel_id=1, source_target_pairs={{0,3},{1,2},{2,1},{3,0},{4,7},{5,6},{6,5},{7,4},{8,11},{9,10},{10,... | collective-permute-start | bytes 184328 | tf_op jit(solution)/shard_map/ppermute | solution.py:473
  12.2 6.5 %collective-permute-start.3 = (f32[240,128]{1,0:T(8,128)S(1)}, f32[240,128]{1,0:T(8,128)S(1)}, u32[]{:S(2)}, u32[]{:S(2)}) collective-permute-start(f32[240,128]{1,0:T(8,128)S(1)} %pack_columns.1.o_ref), channel_id=1, source_target_pairs={{0,28},{4,8},{8,4},{12,16},{16,12},{20,24},{24,20},{28,0},{1,29},{... | collective-permute-start | bytes 368648 | tf_op jit(solution)/shard_map/ppermute | solution.py:473
  13.4 5.4 %collective-permute-start.2 = (f32[240,128]{1,0:T(8,128)S(1)}, f32[240,128]{1,0:T(8,128)S(1)}, u32[]{:S(2)}, u32[]{:S(2)}) collective-permute-start(f32[240,128]{1,0:T(8,128)S(1)} %pack_columns.1.o_ref), channel_id=1, source_target_pairs={{0,4},{4,0},{8,12},{12,8},{16,20},{20,16},{24,28},{28,24},{1,5},{5... | collective-permute-start | bytes 368648 | tf_op jit(solution)/shard_map/ppermute | solution.py:473

commit v3 on v0

v3 whole, which is shorter than its diff:
```python
import jax
import jax.numpy as jnp
from jax import lax
from jax.experimental import pallas as pl
from jax.experimental.pallas import tpu as pltpu
from jax.sharding import PartitionSpec as P

DIFF = 0.15
SHIFT = 4.0
LANES = 128
ROWS = 64
HALO = 8
EXT = ROWS + 2 * HALO
PAD = EXT + 2 * HALO
CHUNKS = EXT // 8
FLOW_AT, MASK_AT, DEPTH_AT, DIAG_AT, MSG_ROWS = 8, 40, 104, 108, 120
DEP, DIA, B, H, U, V, W, HU, HV, HW = range(10)
M0, M1, FU, FV, PDEP, PDIA = range(6)
FIRST, LAST = 4, LANES - 5
PAIRS = ((0, 0), (0, 1), (0, 2), (1, 1), (1, 2), (2, 2))
NSUMS = 5 + 5 * len(PAIRS)
SUM_ROWS = 40


def lane_iota():
    return lax.broadcasted_iota(jnp.int32, (8, LANES), 1)


def roll(x, by):
    by = by % LANES
    return pltpu.roll(x, by, 1) if by else x


def over_groups(x):
    for by in (16, 32, 64):
        x = x + roll(x, by)
    return x


def in_every_group(x, lane):
    return over_groups(jnp.where(lane < 16, x, 0.0))


def message_shift(level):
    return 16 * (level % 8) + 8 * (level // 8) + 4


def own_shift(level):
    return 16 * (level % 8) + 8


def pack_messages(values, lane):
    eighth = lane // 8
    packed = values[0]
    for level, value in enumerate(values):
        turned = roll(value, message_shift(level))
        packed = jnp.where(eighth == 2 * (level % 8) + level // 8, turned, packed) if level else turned
    return packed


def pack_own(values, lane):
    packed = roll(values[0], own_shift(0))
    for level in range(1, 8):
        packed = jnp.where(lane // 16 == level, roll(values[level], own_shift(level)), packed)
    return packed


def pack_surface(depth, diag, lane):
    return in_every_group(jnp.where(lane % 16 < 8, roll(depth, 4), roll(diag, 12)), lane)


def aligned(start, count=8):
    return pl.ds(pl.multiple_of(start, 8), count)


def level_rows(ref, at, count, index, south):
    start = at + count * index
    return ref[pl.ds(start - (8 - count) if south else start, 8), :]


def row_message_kernel(adj, zon, mer, depth, diag, a_ref, b_ref, adj_ref, flow_ref, depth_ref, diag_ref, sems):
    copies = []
    for edge, start in ((0, 0), (1, ROWS - 8)):
        rows = pl.ds(start, 8)
        for source, target in (
            (adj.at[:, rows, :], adj_ref.at[edge]),
            (zon.at[1, :, rows, :], flow_ref.at[edge, 0]),
            (mer.at[1, :, rows, :], flow_ref.at[edge, 1]),
            (depth.at[rows, :], depth_ref.at[edge]),
            (diag.at[rows, :], diag_ref.at[edge]),
        ):
            copies.append(pltpu.make_async_copy(source, target, sems.at[len(copies)]))
            copies[-1].start()
    even = lax.rem(lax.axis_index("lat"), 2) == 0
    zero = jnp.zeros((8, LANES), jnp.float32)
    for ref in (a_ref, b_ref):
        ref[0:8, :] = zero
        ref[MSG_ROWS - 8 : MSG_ROWS, :] = zero
    for copy in copies:
        copy.wait()

    def put(at, low, high):
        count = low.shape[0]
        a_ref[pl.ds(at, count), :] = jnp.where(even, high, low)
        b_ref[pl.ds(at, count), :] = jnp.where(even, low, high)

    depth_low = depth_ref[0, 0:4, :].astype(jnp.float32)
    depth_high = depth_ref[1, 4:8, :].astype(jnp.float32)
    for level in range(16):
        k = float(level % 8)
        low = jnp.where(depth_low > k, adj_ref[0, level, 0:4, :], 0.0)
        high = jnp.where(depth_high > k, adj_ref[1, level, 4:8, :], 0.0)
        put(MASK_AT + 4 * level, low, high)
    put(DEPTH_AT, depth_low, depth_high)
    put(DIAG_AT, diag_ref[0, 0:4, :], diag_ref[1, 4:8, :])
    for level in range(16):
        low = 0.5 * flow_ref[0, level // 8, level % 8].astype(jnp.float32)
        high = 0.5 * flow_ref[1, level // 8, level % 8].astype(jnp.float32)
        put(FLOW_AT + 2 * level, low[0:2], high[6:8])


def sort_rows(recv_a_ref, recv_b_ref, south_ref, north_ref, last):
    lat = lax.axis_index("lat")
    even = lax.rem(lat, 2) == 0
    for start in range(0, MSG_ROWS, 8):
        a = recv_a_ref[pl.ds(start, 8), :]
        b = recv_b_ref[pl.ds(start, 8), :]
        south_ref[pl.ds(start, 8), :] = jnp.where(lat == 0, 0.0, jnp.where(even, b, a))
        north_ref[pl.ds(start, 8), :] = jnp.where(lat == last, 0.0, jnp.where(even, a, b))


def pack_interior_kernel(c_ref, adj_ref, zon_ref, mer_ref, depth_ref, diag_ref, o_ref, own_ref, late_ref, m_ref, f_ref):
    del c_ref
    lane = lane_iota()

    def rows(r, carry):
        at = aligned(8 * r)
        to = aligned(8 * r + HALO)
        depth = depth_ref[at, :].astype(jnp.float32)
        diag = diag_ref[at, :]
        masked = [jnp.where(depth > float(level % 8), adj_ref[level, at, :], 0.0) for level in range(16)]
        flows = [
            0.5 * ref[1, k, at, :].astype(jnp.float32) for ref in (zon_ref, mer_ref) for k in range(8)
        ]
        for level in range(16):
            m_ref[level, aligned(8 * r + 2 * HALO), :] = masked[level]
            f_ref[level, aligned(8 * r + 2 * HALO), :] = flows[level]
        o_ref[to, :] = pack_messages(masked, lane)
        o_ref[aligned(EXT + 8 * r + HALO), :] = pack_messages(flows, lane)
        o_ref[aligned(2 * EXT + 8 * r + HALO), :] = pack_surface(depth, diag, lane)
        own_ref[M0, to, :] = pack_own(masked[:8], lane)
        own_ref[M1, to, :] = pack_own(masked[8:], lane)
        own_ref[FU, to, :] = pack_own(flows[:8], lane)
        own_ref[FV, to, :] = pack_own(flows[8:], lane)
        own_ref[PDEP, to, :] = in_every_group(roll(depth, 8), lane)
        own_ref[PDIA, to, :] = in_every_group(roll(diag, 8), lane)
        for which, ref in enumerate((zon_ref, mer_ref)):
            late_ref[which, at, :] = pack_own([0.5 * ref[0, k, at, :].astype(jnp.float32) for k in range(8)], lane)
        return carry

    lax.fori_loop(0, ROWS // 8, rows, 0)


def make_pack_edges_kernel(last):
    def kernel(ra_ref, rb_ref, o_in_ref, o_ref, south_ref, north_ref):
        del o_in_ref
        sort_rows(ra_ref, rb_ref, south_ref, north_ref, last)
        lane = lane_iota()
        for ref, south, base in ((south_ref, True, 0), (north_ref, False, HALO + ROWS)):
            masked = [level_rows(ref, MASK_AT, 4, level, south) for level in range(16)]
            o_ref[base : base + 8, :] = pack_messages(masked, lane)
            flows = [level_rows(ref, FLOW_AT, 2, level, south) for level in range(16)]
            o_ref[EXT + base : EXT + base + 8, :] = pack_messages(flows, lane)
            depth = level_rows(ref, DEPTH_AT, 4, 0, south)
            diag = level_rows(ref, DIAG_AT, 4, 0, south)
            o_ref[2 * EXT + base : 2 * EXT + base + 8, :] = pack_surface(depth, diag, lane)

    return kernel


def rows_at(r, shift=0):
    start = HALO + 8 * r
    return pl.ds(pl.multiple_of(start, 8) if shift == 0 else start + shift, 8)


def star(ref, r):
    centre = ref[rows_at(r), :]
    return centre, roll(centre, 1), roll(centre, -1), ref[rows_at(r, -1), :], ref[rows_at(r, 1), :]


def shifted(ref, diag_ref, r):
    centre, west, east, south, north = star(ref, r)
    return diag_ref[rows_at(r), :] * centre - (west + east + south + north)


def on_grid(r, last, value):
    lat = lax.axis_index("lat")
    at = 8 * r + lax.broadcasted_iota(jnp.int32, (8, LANES), 0) - HALO
    beyond = ((at < 0) & (lat == 0)) | ((at >= ROWS) & (lat == last))
    return jnp.where(beyond, 0.0, value)


def apply(coef, centre, west, east, south, north):
    c0, cw, ce, cs, cn = coef
    return (c0 * centre + cw * west) + (ce * east + cs * south) + cn * north


def coefficients(u, w, mins, k):
    dep, dw, de, ds, dn = mins
    cw = jnp.where(dw > k, DIFF - u, 0.0)
    ce = jnp.where(de > k, DIFF + u, 0.0)
    cs = jnp.where(ds > k, DIFF - w, 0.0)
    cn = jnp.where(dn > k, DIFF + w, 0.0)
    c0 = jnp.where(dep > k, 1.0 - ((cw + ce) + (cs + cn)), 0.0)
    return c0, cw, ce, cs, cn


def depths(ref, r):
    dep, *others = star(ref, r)
    return [dep] + [jnp.minimum(dep, d) for d in others]


def products(b, h, hh, fields, image, second):
    new = [b * b, b * h, h * h, h * hh, b * hh]
    for left, right in ((fields, fields), (fields, image), (image, image), (image, second), (fields, second)):
        for i, j in PAIRS:
            if i == j or left is right:
                new.append(left[i] * right[j])
            else:
                new.append(left[i] * right[j] + left[j] * right[i])
    return new


def make_block_kernel(last):
    def kernel(
        c_ref, depth_ref, diag_ref, ra_ref, rb_ref, own_in_ref, m_in_ref, f_in_ref,
        am_ref, pq_ref, s_ref, sums_ref, shift_ref, own_ref, m_ref, f_ref,
        south_ref, north_ref,
    ):
        del own_in_ref, m_in_ref, f_in_ref
        lane = lane_iota()
        coup = [c_ref[level // 8, level % 8] for level in range(16)]
        square = [coup[k] * coup[k] + coup[k + 8] * coup[k + 8] for k in range(8)]
        sort_rows(ra_ref, rb_ref, south_ref, north_ref, last)
        lo, hi, mid = HALO, EXT, 2 * HALO
        for level in range(16):
            for ref, at, count in ((m_ref, MASK_AT, 4), (f_ref, FLOW_AT, 2)):
                ref[level, lo : lo + 8, :] = level_rows(south_ref, at, count, level, True)
                ref[level, hi : hi + 8, :] = level_rows(north_ref, at, count, level, False)
        for field, at in ((DEP, DEPTH_AT), (DIA, DIAG_AT)):
            s_ref[field, lo : lo + 8, :] = level_rows(south_ref, at, 4, 0, True)
            s_ref[field, hi : hi + 8, :] = level_rows(north_ref, at, 4, 0, False)

        s_ref[DEP, mid : mid + ROWS, :] = depth_ref[...].astype(jnp.float32)
        s_ref[DIA, mid : mid + ROWS, :] = diag_ref[...]

        def rhs(r, carry):
            at = rows_at(r)
            parts = [coup[level] * m_ref[level, at, :] for level in range(16)]
            while len(parts) > 1:
                parts = [parts[i] + parts[i + 1] for i in range(0, len(parts), 2)]
            s_ref[B, at, :] = parts[0]
            return carry

        lax.fori_loop(0, CHUNKS, rhs, 0)

        zero = jnp.zeros((8, LANES), jnp.float32)

        def quotient(r, carry):
            b = s_ref[B, rows_at(r), :]
            return carry[0] + b * b, carry[1] + b * shifted(s_ref.at[B], s_ref.at[DIA], r)

        squares, images_sum = lax.fori_loop(1, CHUNKS - 1, quotient, (zero, zero), unroll=2)
        inside = (lane > 0) & (lane < LANES - 1)
        squares, images_sum = [
            jnp.sum(jnp.sum(jnp.where(inside, v, 0.0), axis=0, keepdims=True), axis=1, keepdims=True)
            for v in (squares, images_sum)
        ]
        shift = jnp.where(squares > 0.0, images_sum / jnp.where(squares > 0.0, squares, 1.0), 0.0)
        shift = jnp.broadcast_to(jnp.clip(shift, -4.0, 5.0), (8, LANES))
        shift_ref[...] = shift

        def images(r, carry):
            s_ref[DIA, rows_at(r), :] = s_ref[DIA, rows_at(r), :] - shift
            s_ref[H, rows_at(r), :] = on_grid(r, last, shifted(s_ref.at[B], s_ref.at[DIA], r))
            return carry

        lax.fori_loop(0, CHUNKS, images, 0, unroll=2)

        def advect(r, carry):
            out_at = aligned(8 * r)
            at, below, above = rows_at(r), rows_at(r, -1), rows_at(r, 1)
            mins = depths(s_ref.at[DEP], r)
            bs = star(s_ref.at[B], r)
            hs = star(s_ref.at[H], r)
            us = vs = ws = jnp.zeros((8, LANES), jnp.float32)
            for k in range(8):
                coef = coefficients(f_ref[k, at, :], f_ref[8 + k, at, :], mins, float(k))
                for level in (k, k + 8):
                    centre = m_ref[level, at, :]
                    value = apply(
                        coef, centre, roll(centre, 1), roll(centre, -1),
                        m_ref[level, below, :], m_ref[level, above, :],
                    )
                    am_ref[level, out_at, :] = value
                    us = us + coup[level] * value
                p = apply(coef, *bs)
                q = apply(coef, *hs)
                pq_ref[k, out_at, :] = p
                pq_ref[8 + k, out_at, :] = q
                vs = vs + square[k] * p
                ws = ws + square[k] * q
            s_ref[U, at, :] = us
            s_ref[V, at, :] = vs
            s_ref[W, at, :] = ws
            return carry

        lax.fori_loop(0, CHUNKS, advect, 0)

        def images_two(r, carry):
            for source, target in ((U, HU), (V, HV), (W, HW)):
                s_ref[target, rows_at(r), :] = on_grid(r, last, shifted(s_ref.at[source], s_ref.at[DIA], r))
            return carry

        lax.fori_loop(0, CHUNKS, images_two, 0, unroll=2)

        def gather(r, sums):
            at = rows_at(r)
            hh, *second = [shifted(s_ref.at[field], s_ref.at[DIA], r) for field in (H, HU, HV, HW)]
            b, h, *rest = [s_ref[field, at, :] for field in (B, H, U, V, W, HU, HV, HW)]
            return tuple(s + n for s, n in zip(sums, products(b, h, hh, rest[:3], rest[3:], second)))

        sums = lax.fori_loop(1, CHUNKS - 1, gather, (zero,) * NSUMS)
        keep = (lane >= FIRST) & (lane <= LAST)
        for index, value in enumerate(sums):
            sums_ref[8 * index : 8 * index + 8, :] = jnp.where(keep, value, 0.0)

        for ref, south, base in ((south_ref, True, 0), (north_ref, False, HALO + ROWS)):
            rows = pl.ds(base, 8)
            for slot, at, count in ((M0, MASK_AT, 4), (FU, FLOW_AT, 2)):
                values = [level_rows(ref, at, count, level, south) for level in range(16)]
                own_ref[slot, rows, :] = pack_own(values[:8], lane)
                own_ref[slot + 1, rows, :] = pack_own(values[8:], lane)
            for slot, at in ((PDEP, DEPTH_AT), (PDIA, DIAG_AT)):
                own_ref[slot, rows, :] = in_every_group(roll(level_rows(ref, at, 4, 0, south), 8), lane)

    return kernel


def group_factors(c_ref, lane):
    first = second = jnp.zeros((8, LANES), jnp.float32)
    for k in range(8):
        first = jnp.where(lane // 16 == k, c_ref[0, k], first)
        second = jnp.where(lane // 16 == k, c_ref[1, k], second)
    return first, second


def make_sides_kernel(last, devices):
    def kernel(
        c_ref, own_ref, pa_ref, pb_ref, block_sums_ref, shift_ref, z_ref, s_ref, sums_ref, m_ref, f_ref, all_ref
    ):
        lane = lane_iota()
        pos = lane % 16
        level_of = (lane // 16).astype(jnp.float32)
        first, second = group_factors(c_ref, lane)
        square = first * first + second * second
        even_lon = lax.rem(lax.axis_index("lon"), 2) == 0
        shift = shift_ref[...]

        def assemble(r, carry):
            at = rows_at(r)
            own_at = aligned(8 * r)
            for side in range(2):
                outer = pos >= 8 if side == 0 else pos < 8
                for part in range(3):
                    src = aligned(part * EXT + 8 * r)
                    a, b = pa_ref[src, :], pb_ref[src, :]
                    got = jnp.where(even_lon, a, b) if side == 0 else jnp.where(even_lon, b, a)
                    one = jnp.where(outer, roll(got, 4), own_ref[2 * part, own_at, :])
                    two = jnp.where(outer, roll(got, -4), own_ref[2 * part + 1, own_at, :])
                    if part == 0:
                        m_ref[side, 0, at, :] = one
                        m_ref[side, 1, at, :] = two
                        s_ref[side, B, at, :] = over_groups(first * one + second * two)
                    elif part == 1:
                        f_ref[side, 0, at, :] = one
                        f_ref[side, 1, at, :] = two
                    else:
                        s_ref[side, DEP, at, :] = one
                        s_ref[side, DIA, at, :] = two - shift
            return carry

        lax.fori_loop(0, CHUNKS, assemble, 0, unroll=10)

        def images(r, carry):
            for side in range(2):
                value = shifted(s_ref.at[side, B], s_ref.at[side, DIA], r)
                s_ref[side, H, rows_at(r), :] = on_grid(r, last, value)
            return carry

        lax.fori_loop(0, CHUNKS, images, 0, unroll=10)

        def advect(r, carry):
            at, out_at = rows_at(r), aligned(8 * r)
            for side in range(2):
                mins = depths(s_ref.at[side, DEP], r)
                coef = coefficients(f_ref[side, 0, at, :], f_ref[side, 1, at, :], mins, level_of)
                one = apply(coef, *star(m_ref.at[side, 0], r))
                two = apply(coef, *star(m_ref.at[side, 1], r))
                p = apply(coef, *star(s_ref.at[side, B], r))
                q = apply(coef, *star(s_ref.at[side, H], r))
                for slot, value in enumerate((one, two, p, q)):
                    z_ref[side, slot, out_at, :] = value
                s_ref[side, U, at, :] = over_groups(first * one + second * two)
                s_ref[side, V, at, :] = over_groups(square * p)
                s_ref[side, W, at, :] = over_groups(square * q)
            return carry

        lax.fori_loop(0, CHUNKS, advect, 0, unroll=5)

        def images_two(r, carry):
            for side in range(2):
                for source, target in ((U, HU), (V, HV), (W, HW)):
                    value = shifted(s_ref.at[side, source], s_ref.at[side, DIA], r)
                    s_ref[side, target, rows_at(r), :] = on_grid(r, last, value)
            return carry

        lax.fori_loop(0, CHUNKS, images_two, 0, unroll=5)

        east = lane < 8

        def gather(r, sums):
            at = rows_at(r)

            def both(field):
                return jnp.where(east, s_ref[0, field, at, :], s_ref[1, field, at, :])

            def image(field):
                one, two = [shifted(s_ref.at[side, field], s_ref.at[side, DIA], r) for side in range(2)]
                return jnp.where(east, one, two)

            hh, *second_image = [image(field) for field in (H, HU, HV, HW)]
            b, h, *rest = [both(field) for field in (B, H, U, V, W, HU, HV, HW)]
            return tuple(s + n for s, n in zip(sums, products(b, h, hh, rest[:3], rest[3:], second_image)))

        zero = jnp.zeros((8, LANES), jnp.float32)
        sums = lax.fori_loop(1, CHUNKS - 1, gather, (zero,) * NSUMS, unroll=1)
        keep = (lane >= 4) & (lane < 12)
        for index, value in enumerate(sums):
            at = pl.ds(8 * index, 8)
            all_ref[at, :] = block_sums_ref[at, :] + jnp.where(keep, value, 0.0)
        for index in range(NSUMS, SUM_ROWS):
            all_ref[pl.ds(8 * index, 8), :] = zero
        row = lax.broadcasted_iota(jnp.int32, (8, LANES), 0)
        line = jnp.zeros((8, LANES), jnp.float32)
        for base in range(0, SUM_ROWS, 8):
            total = all_ref[pl.ds(8 * base, 8, stride=8), :]
            for sub in range(1, 8):
                total = total + all_ref[pl.ds(8 * base + sub, 8, stride=8), :]
            total = jnp.sum(total, axis=1, keepdims=True)
            line = jnp.where(lane == base + row, total, line)
        line = jnp.sum(line, axis=0, keepdims=True)
        line = jnp.where(lane[0:1, :] == NSUMS, shift[0:1, :], line)
        sums_ref[...] = jnp.broadcast_to(line, (devices, LANES))

    return kernel


def solve(m0, m1, m2, m3, m4, shift):
    def over_devices(x):
        return jnp.sum(x, axis=1, keepdims=True)

    norm = over_devices(m0)
    mean = over_devices(m1 + shift * m0) / norm
    theta = mean + SHIFT
    delta = shift - mean
    spread = over_devices(m2 + delta * (2.0 * m1 + delta * m0))
    curve = over_devices(m3 + delta * (2.0 * m2 + m4 + delta * (3.0 * m1 + delta * m0)))
    ratio = spread / (theta * theta * norm)
    gamma = curve / spread + theta * (1.0 - ratio)
    image = -1.0 / (theta * gamma)
    return 1.0 / theta + ratio / gamma + delta * image, image


def make_finish_kernel(lat_count):
    def kernel(
        c_ref, zon_ref, mer_ref, am_ref, pq_ref, s_ref, late_ref, z_ref, side_ref, sums_ref,
        out_ref, sens_ref, m_ref, zm_ref, zx_ref,
    ):
        lane = lane_iota()
        pos = lane % 16
        level_of = (lane // 16).astype(jnp.float32)
        coup = [c_ref[level // 8, level % 8] for level in range(16)]
        first, second = group_factors(c_ref, lane)

        devices = sums_ref.shape[0]
        blocks = []
        for base in range(0, devices, LANES):
            part = sums_ref[base : min(base + LANES, devices), :]
            if part.shape[0] < LANES:
                part = jnp.concatenate([part, jnp.zeros((LANES - part.shape[0], LANES), jnp.float32)], axis=0)
            blocks.append(jnp.transpose(part))
        turned = blocks[0] if len(blocks) == 1 else jnp.concatenate(blocks, axis=1)
        rows = [turned[i : i + 1, :] for i in range(NSUMS + 1)]
        shift = rows[NSUMS]
        near, e1 = solve(*rows[:5], shift)
        factor = (None, near, e1, near * near, near * e1, e1 * e1)
        moments = []
        for kind in range(5):
            base = 5 + kind * len(PAIRS)
            value = rows[base]
            for index in range(1, len(PAIRS)):
                twice = 2.0 if kind in (0, 2) and index in (1, 2, 4) else 1.0
                value = value + (twice * factor[index]) * rows[base + index]
            moments.append(value)
        late, e0 = solve(*moments, shift)
        me = lax.axis_index("lon") * lat_count + lax.axis_index("lat")
        mine = lax.broadcasted_iota(jnp.int32, shift.shape, 1) == me
        a1, a0 = [jnp.sum(jnp.where(mine, v, 0.0), axis=1, keepdims=True) for v in (near, late)]
        a1, e1, a0, e0 = [jnp.broadcast_to(v, (8, LANES)) for v in (a1, e1, a0, e0)]

        def surface(ref, at):
            b = ref[U, at, :] + a1 * ref[V, at, :] + e1 * ref[W, at, :]
            h = ref[HU, at, :] + a1 * ref[HV, at, :] + e1 * ref[HW, at, :]
            x = a0 * b + e0 * h
            return x, x + (a1 * ref[B, at, :] + e1 * ref[H, at, :])

        def middle(r, carry):
            at, to = aligned(8 * r), rows_at(r)
            for side in range(2):
                x, both_steps = surface(side_ref.at[side], to)
                zx_ref[side, at, :] = both_steps
                part = a1 * z_ref[side, 2, at, :] + e1 * z_ref[side, 3, at, :]
                part = part + jnp.where(side_ref[side, DEP, to, :] > level_of, x, 0.0)
                zm_ref[side, 0, to, :] = z_ref[side, 0, at, :] + first * part
                zm_ref[side, 1, to, :] = z_ref[side, 1, at, :] + second * part
            x, both_steps = surface(s_ref, to)
            zx_ref[2, at, :] = both_steps
            dep = s_ref[DEP, to, :]
            for k in range(8):
                part = a1 * pq_ref[k, at, :] + e1 * pq_ref[8 + k, at, :] + jnp.where(dep > float(k), x, 0.0)
                for level in (k, k + 8):
                    m_ref[level, to, :] = am_ref[level, at, :] + coup[level] * part
            return carry

        lax.fori_loop(0, CHUNKS, middle, 0, unroll=2)

        edge = (lane < FIRST) | (lane > LAST)

        def advect(i, carry):
            r = i + 1
            out_at = aligned(8 * i)
            ext_at = aligned(8 * r)
            at, below, above = rows_at(r), rows_at(r, -1), rows_at(r, 1)
            sides = []
            for side in range(2):
                mins = depths(side_ref.at[side, DEP], r)
                coef = coefficients(late_ref[0, out_at, :], late_ref[1, out_at, :], mins, level_of)
                sides.append([apply(coef, *star(zm_ref.at[side, t], r)) for t in range(2)])
            inserts = [jnp.where(pos < 8, sides[0][t], sides[1][t]) for t in range(2)]
            ins = jnp.where(pos < 8, zx_ref[0, ext_at, :], zx_ref[1, ext_at, :])
            sens_ref[out_at, :] = jnp.where(edge, roll(ins, -8), zx_ref[2, ext_at, :])
            mins = depths(s_ref.at[DEP], r)
            for k in range(8):
                u = 0.5 * zon_ref[0, k, out_at, :].astype(jnp.float32)
                w = 0.5 * mer_ref[0, k, out_at, :].astype(jnp.float32)
                coef = coefficients(u, w, mins, float(k))
                for level in (k, k + 8):
                    centre = m_ref[level, at, :]
                    value = apply(
                        coef, centre, roll(centre, 1), roll(centre, -1),
                        m_ref[level, below, :], m_ref[level, above, :],
                    )
                    value = jnp.where(edge, roll(inserts[level // 8], -own_shift(k)), value)
                    out_ref[level, out_at, :] = value
            return carry

        lax.fori_loop(0, ROWS // 8, advect, 0, unroll=2)

    return kernel


VMEM = pl.BlockSpec(memory_space=pltpu.VMEM)
HBM = pl.BlockSpec(memory_space=pltpu.HBM)


def on_device_of(lon, lat):
    devices = lon * lat
    f32 = jnp.float32

    def array(*shape):
        return jax.ShapeDtypeStruct(shape, f32)

    smem = pl.BlockSpec(memory_space=pltpu.SMEM)
    params = pltpu.CompilerParams(vmem_limit_bytes=48 * 2**20)
    pairs = {}
    for axis, count in (("lon", lon), ("lat", lat)):
        first = [(i, i ^ 1) for i in range(count)]
        second = [(i, (i - 1) % count if i % 2 == 0 else (i + 1) % count) for i in range(count)]
        pairs[axis] = (first, second)

    def swap(axis, a, b):
        first, second = pairs[axis]
        return lax.ppermute(a, axis, first), lax.ppermute(b, axis, second)

    def on_device(adj_tracer, zonal_flow, meridional_flow, depth, coupling, surface_diag):
        adj = adj_tracer.reshape(16, ROWS, LANES)
        block_args = (adj, zonal_flow, meridional_flow, depth, surface_diag)
        msg_a, msg_b = pl.pallas_call(
            row_message_kernel,
            in_specs=[HBM] * 5,
            out_specs=[VMEM] * 2,
            out_shape=[array(MSG_ROWS, LANES)] * 2,
            scratch_shapes=[
                pltpu.VMEM((2, 16, 8, LANES), f32),
                pltpu.VMEM((2, 2, 8, 8, LANES), jnp.bfloat16),
                pltpu.VMEM((2, 8, LANES), jnp.int32),
                pltpu.VMEM((2, 8, LANES), f32),
                pltpu.SemaphoreType.DMA((10,)),
            ],
            compiler_params=pltpu.CompilerParams(vmem_limit_bytes=62914560),
            name="row_messages",
        )(*block_args)
        recv_a, recv_b = swap("lat", msg_a, msg_b)
        packed, own, late, masked, flows = pl.pallas_call(
            pack_interior_kernel,
            in_specs=[smem] + [VMEM] * 5,
            out_specs=[VMEM] * 5,
            out_shape=[
                array(3 * EXT, LANES), array(6, EXT, LANES), array(2, ROWS, LANES),
                array(16, PAD, LANES), array(16, PAD, LANES),
            ],
            compiler_params=params,
            cost_estimate=pl.CostEstimate(flops=4_000_000, bytes_accessed=1_000_000, transcendentals=0),
            name="pack_interior",
        )(coupling, *block_args)
        row_scratch = [pltpu.VMEM((MSG_ROWS, LANES), f32)] * 2
        packed = pl.pallas_call(
            make_pack_edges_kernel(lat - 1),
            in_specs=[VMEM] * 3,
            out_specs=VMEM,
            out_shape=array(3 * EXT, LANES),
            scratch_shapes=row_scratch,
            input_output_aliases={2: 0},
            compiler_params=params,
            name="pack_edges",
        )(recv_a, recv_b, packed)
        side_a, side_b = swap("lon", packed, packed)
        am, pq, block, block_sums, shift, own, _, _ = pl.pallas_call(
            make_block_kernel(lat - 1),
            in_specs=[smem] + [VMEM] * 7,
            out_specs=[VMEM] * 8,
            out_shape=[
                array(16, EXT, LANES), array(16, EXT, LANES), array(10, PAD, LANES),
                array(8 * NSUMS, LANES), array(8, LANES), array(6, EXT, LANES),
                array(16, PAD, LANES), array(16, PAD, LANES),
            ],
            scratch_shapes=row_scratch,
            input_output_aliases={5: 5, 6: 6, 7: 7},
            compiler_params=params,
            cost_estimate=pl.CostEstimate(flops=16_000_000, bytes_accessed=4_000_000, transcendentals=0),
            name="block",
        )(coupling, depth, surface_diag, recv_a, recv_b, own, masked, flows)
        z, sides, sums = pl.pallas_call(
            make_sides_kernel(lat - 1, devices),
            in_specs=[smem] + [VMEM] * 5,
            out_specs=[VMEM] * 3,
            out_shape=[array(2, 4, EXT, LANES), array(2, 10, PAD, LANES), array(devices, LANES)],
            scratch_shapes=[
                pltpu.VMEM((2, 2, PAD, LANES), f32),
                pltpu.VMEM((2, 2, PAD, LANES), f32),
                pltpu.VMEM((8 * SUM_ROWS, LANES), f32),
            ],
            compiler_params=params,
            name="sides",
        )(coupling, own, side_a, side_b, block_sums, shift)
        everyone = lax.all_to_all(sums, ("lon", "lat"), 0, 0, tiled=True)
        out, sens = pl.pallas_call(
            make_finish_kernel(lat),
            in_specs=[smem] + [VMEM] * 9,
            out_specs=[VMEM] * 2,
            out_shape=[array(16, ROWS, LANES), array(ROWS, LANES)],
            scratch_shapes=[
                pltpu.VMEM((16, PAD, LANES), f32),
                pltpu.VMEM((2, 2, PAD, LANES), f32),
                pltpu.VMEM((3, EXT, LANES), f32),
            ],
            compiler_params=params,
            name="finish",
        )(coupling, zonal_flow, meridional_flow, am, pq, block, late, z, sides, everyone)
        return out.reshape(adj_tracer.shape), sens

    return on_device


def solution(mesh):
    in_specs = (
        P(None, None, "lat", "lon"),
        P(None, None, "lat", "lon"),
        P(None, None, "lat", "lon"),
        P("lat", "lon"),
        P(),
        P("lat", "lon"),
    )
    out_specs = (P(None, None, "lat", "lon"), P("lat", "lon"))
    return jax.shard_map(
        on_device_of(mesh.shape["lon"], mesh.shape["lat"]),
        mesh=mesh, in_specs=in_specs, out_specs=out_specs, check_vma=False,
    )
```

time: 366 us -> 35.7 us (0.10)
  blocking collectives: 239 us -> 10.2 us
  starting transfers between devices: 43.2 us -> 8.16 us
  local copies, waits for them, and re-layouts: 32.5 us -> 0.03 us
  other arithmetic: 25.3 us -> 0 us
  Pallas kernels: 0 us -> 15.5 us
  waiting for transfers between devices: 14.1 us -> 0.89 us
  between operations: 9 us -> 0.74 us
    psum x6 -> x0, blocking collectives: 239 us -> none  [the longest x4 160 us: global_squares(): return lax.psum(jnp.sum(residual * residual), ('lon', 'lat'))]
    ppermute x24 -> x4, starting transfers between devices: 43.2 us -> 8.16 us  [swap(): return (lax.ppermute(a, axis, first), lax.ppermute(b, axis, second))]
    pallas_call x0 -> x6, Pallas kernels: none -> 15.5 us  [the longest x1 4.21 us: on_device(): pl.pallas_call(make_block_kernel(lat - 1), in_specs=[smem] + [VMEM] * 7,...]
    concatenate x8 -> x0, other arithmetic: 14 us -> none  [the longest x4 7.7 us: padded(): jnp.concatenate([lax.ppermute(tail, axis, [(i, (i + 1) % count) for i in...]
    ppermute x24 -> x4, waiting for transfers between devices: 14.1 us -> 0.89 us  [swap(): return (lax.ppermute(a, axis, first), lax.ppermute(b, axis, second))]
    slice x14 -> x0, local copies, waits for them, and re-layouts: 11.6 us -> none  [the longest x10 5.33 us: padded(): lax.slice_in_dim(cells, cells.shape[dim] - width, cells.shape[dim], axis=...]
    unnamed x53 -> x12, local copies, waits for them, and re-layouts: 11.3 us -> 0.03 us
    all_to_all x0 -> x1, blocking collectives: none -> 10.2 us  [on_device(): everyone = lax.all_to_all(sums, ('lon', 'lat'), 0, 0, tiled=True)]
  transfers between devices with their start and end apart: 24 -> 4, of which waited for: 8 -> 1; matrix products, arithmetic and copies ran while one was open for 7% -> 0% of each run, Pallas kernels for 0% -> 20%
where the time goes in v3:
time: 35.7 us; the launch traced here: 35.6 us
  Pallas kernels  15.5 us (43%)
  blocking collectives  10.2 us (29%)
  starting transfers between devices  8.16 us (23%)
  waiting for transfers between devices  0.89 us (2%)
  between operations  0.74 us (2%)
    all_to_all x1, blocking collectives, on_device(): everyone = lax.all_to_all(sums, ('lon', 'lat'), 0, 0, tiled=True)  10.2 us
    ppermute x4, starting transfers between devices, swap(): return (lax.ppermute(a, axis, first), lax.ppermute(b, axis, second))  8.16 us
    pallas_call x1, Pallas kernels, on_device(): pl.pallas_call(make_block_kernel(lat - 1), in_specs=[smem] + [VMEM] * 7,...  4.21 us
    pallas_call x1, Pallas kernels, on_device(): pl.pallas_call(make_finish_kernel(lat), in_specs=[smem] + [VMEM] * 9, out...  3.43 us
    pallas_call x1, Pallas kernels, on_device(): pl.pallas_call(make_sides_kernel(lat - 1, devices), in_specs=[smem] + [VM...  2.99 us
    pallas_call x1, Pallas kernels, on_device(): pl.pallas_call(pack_interior_kernel, in_specs=[smem] + [VMEM] * 5, out_sp...  2.83 us
    pallas_call x1, Pallas kernels, on_device(): pl.pallas_call(row_message_kernel, in_specs=[HBM] * 5, out_specs=[VMEM] *...  1.76 us
    ppermute x4, waiting for transfers between devices, swap(): return (lax.ppermute(a, axis, first), lax.ppermute(b, axis, second))  0.89 us
  transfers between devices with their start and end apart: 4, of which 1 were waited for; matrix products, arithmetic and copies ran while one was open for 0% of the time, Pallas kernels for 20%

profile of v3, /device:TPU:0, one launch (start us, length us, event | category | flops | bytes accessed | tf_op | source)
XLA Modules:
  0.0 35.6 jit_solution(884846629892191271)
XLA Ops:
  0.6 0.0 copy-start
  0.6 0.0 copy-start.1
  0.7 0.0 copy-start.2
  0.7 0.0 copy-start.3
  0.7 0.0 copy-start.4
  0.7 1.8 %row_messages.1 = (f32[120,128]{1,0:T(8,128)}, f32[120,128]{1,0:T(8,128)}) custom-call(f32[16,64,128]{2,1,0:T(8,128)} %bitcast.6, bf16[2,8,64,128]{3,2,1,0:T(8,128)(2,1)} %zon_ref.3, bf16[2,8,64,128]{3,2,1,0:T(8,128)(2,1)} %mer_ref.3, s32[64,128]{1,0:T(8,128)} %depth_ref.3, f32[64,128]{1,0:T(8,128)} %diag_ref.3), custom_call_target="tpu_custom_call" | custom-call | tf_op jit(solution)/shard_map/row_messages/pallas_call | solution.py:609
  2.4 0.0 copy-start.5
  2.5 3.1 %collective-permute-start = (f32[120,128]{1,0:T(8,128)}, f32[120,128]{1,0:T(8,128)S(1)}, u32[]{:S(2)}, u32[]{:S(2)}) collective-permute-start(f32[120,128]{1,0:T(8,128)} %get-tuple-element.20), channel_id=1, source_target_pairs={{0,1},{1,0},{2,3},{3,2},{4,5},{5,4},{6,7},{7,6},{8,9},{9,8},{10,11... | collective-permute-start | bytes 184328 | tf_op jit(solution)/shard_map/ppermute | solution.py:604
  5.5 2.5 %collective-permute-start.1 = (f32[120,128]{1,0:T(8,128)}, f32[120,128]{1,0:T(8,128)S(1)}, u32[]{:S(2)}, u32[]{:S(2)}) collective-permute-start(f32[120,128]{1,0:T(8,128)} %get-tuple-element.21), channel_id=1, source_target_pairs={{0,3},{1,2},{2,1},{3,0},{4,7},{5,6},{6,5},{7,4},{8,11},{9,10},{10,... | collective-permute-start | bytes 184328 | tf_op jit(solution)/shard_map/ppermute | solution.py:604
  8.0 0.0 copy-done
  8.0 0.0 copy-done.4
  8.0 0.0 copy-done.5
  8.1 2.8 %pack_interior.1 = (f32[240,128]{1,0:T(8,128)S(1)}, f32[6,80,128]{2,1,0:T(8,128)S(1)}, f32[2,64,128]{2,1,0:T(8,128)S(1)}, f32[16,96,128]{2,1,0:T(8,128)S(1)}, f32[16,96,128]{2,1,0:T(8,128)S(1)}) custom-call(f32[2,8]{1,0:T(2,128)S(1)} %copy-done.5, f32[16,64,128]{2,1,0:T(8,128)S(1)} %bitcast.7, bf16[2,8,64,128]{3,2,1,0:T(8,128)(2,1)S(1)} %copy-done, ...), custom_call_target="tpu_custom_call" | custom-call | flops 4000000 | bytes 1000000 | tf_op jit(solution)/shard_map/pack_interior/pallas_call | solution.py:625
  10.9 0.0 collective-permute-done.ra_ref
  10.9 0.9 %collective-permute-done.1.rb_ref = f32[120,128]{1,0:T(8,128)S(1)} collective-permute-done((f32[120,128]{1,0:T(8,128)}, f32[120,128]{1,0:T(8,128)S(1)}, u32[]{:S(2)}, u32[]{:S(2)}) %collective-permute-start.1) | collective-permute-done | bytes 61472 | tf_op jit(solution)/shard_map/ppermute | solution.py:604
  11.8 0.3 pack_edges.1
  12.1 0.0 collective-permute-start.2
  12.1 2.5 %collective-permute-start.3 = (f32[240,128]{1,0:T(8,128)S(1)}, f32[240,128]{1,0:T(8,128)S(1)}, u32[]{:S(2)}, u32[]{:S(2)}) collective-permute-start(f32[240,128]{1,0:T(8,128)S(1)} %pack_edges.1), channel_id=1, source_target_pairs={{0,28},{4,8},{8,4},{12,16},{16,12},{20,24},{24,20},{28,0},{1,29},{... | collective-permute-start | bytes 368648 | tf_op jit(solution)/shard_map/ppermute | solution.py:604
  14.7 4.2 %block.1 = (f32[16,80,128]{2,1,0:T(8,128)S(1)}, f32[16,80,128]{2,1,0:T(8,128)S(1)}, f32[10,96,128]{2,1,0:T(8,128)S(1)}, f32[280,128]{1,0:T(8,128)S(1)}, f32[8,12...) custom-call(f32[2,8]{1,0:T(2,128)S(1)} %copy-done.5, ...), custom_call_target="tpu_custom_call", output_to_operand_aliasing={{5}: (5, {}), {6}: (6, {}), {7}: (7, {})} | custom-call | flops 16000000 | bytes 4000000 | tf_op jit(solution)/shard_map/block/pallas_call | solution.py:649
  18.9 0.0 collective-permute-done.2.pa_ref
  18.9 0.0 collective-permute-done.3.pb_ref
  18.9 3.0 %sides.1 = (f32[2,4,80,128]{3,2,1,0:T(8,128)S(1)}, f32[2,10,96,128]{3,2,1,0:T(8,128)S(1)}, f32[32,128]{1,0:T(8,128)S(1)}) custom-call(f32[2,8]{1,0:T(2,128)S(1)} %copy-done.5, f32[6,80,128]{2,1,0:T(8,128)S(1)} %get-tuple-element.29.own_ref, f32[240,128]{1,0:T(8,128)S(1)} %collective-permute-done.2.pa_ref, f32[240,128]{1,0:T(8,128)S(1)} %collective-permute-done.3.pb_ref, ...), custom_call_target="tpu_custom_call" | custom-call | tf_op jit(solution)/shard_map/sides/pallas_call | solution.py:664
  21.9 10.2 %all_to_all.11 = f32[32,1,128]{2,1,0:T(1,128)S(1)} all-to-all(f32[32,1,128]{2,1,0:T(1,128)S(1)} %bitcast.9), channel_id=1, replica_groups=mesh['lon'=8,'lat'=4] {'lon','lat'}, dimensions={0} | all-to-all | bytes 32768 | tf_op jit(solution)/shard_map/all_to_all | solution.py:677
  32.1 3.4 %finish.1 = (f32[16,64,128]{2,1,0:T(8,128)}, f32[64,128]{1,0:T(8,128)}) custom-call(f32[2,8]{1,0:T(2,128)S(1)} %copy-done.5, bf16[2,8,64,128]{3,2,1,0:T(8,128)(2,1)S(1)} %copy-done, bf16[2,8,64,128]{3,2,1,0:T(8,128)(2,1)S(1)} %copy-done.1, f32[16,80,128]{2,1,0:T(8,128)S(1)} %get-tuple-element.25.am_ref, f32[16,80,128]{2,1,0:T(8,128)S(1)} %get-tuple-element.26.pq_ref, ...), custom_call_target="tpu_custom_call" | custom-call | tf_op jit(solution)/shard_map/finish/pallas_call | solution.py:678
  (3 shorter events, 0.0 us)
Async XLA Ops:
  0.6 7.4 %copy-start = (bf16[2,8,64,128]{3,2,1,0:T(8,128)(2,1)S(1)}, bf16[2,8,64,128]{3,2,1,0:T(8,128)(2,1)}, u32[]{:S(2)}) copy-start(bf16[2,8,64,128]{3,2,1,0:T(8,128)(2,1)} %zon_ref.3) | copy-start | bytes 786436
  0.6 7.4 %copy-start.1 = (bf16[2,8,64,128]{3,2,1,0:T(8,128)(2,1)S(1)}, bf16[2,8,64,128]{3,2,1,0:T(8,128)(2,1)}, u32[]{:S(2)}) copy-start(bf16[2,8,64,128]{3,2,1,0:T(8,128)(2,1)} %mer_ref.3) | copy-start | bytes 786436
  0.7 7.4 %copy-start.2 = (f32[2,8,64,128]{3,2,1,0:T(8,128)S(1)}, f32[2,8,64,128]{3,2,1,0:T(8,128)}, u32[]{:S(2)}) copy-start(f32[2,8,64,128]{3,2,1,0:T(8,128)} %param.6) | copy-start | bytes 1572868
  0.7 7.4 %copy-start.3 = (s32[64,128]{1,0:T(8,128)S(1)}, s32[64,128]{1,0:T(8,128)}, u32[]{:S(2)}) copy-start(s32[64,128]{1,0:T(8,128)} %depth_ref.3) | copy-start | bytes 98308
  0.7 7.4 %copy-start.4 = (f32[64,128]{1,0:T(8,128)S(1)}, f32[64,128]{1,0:T(8,128)}, u32[]{:S(2)}) copy-start(f32[64,128]{1,0:T(8,128)} %diag_ref.3) | copy-start | bytes 98308
  2.4 5.6 %copy-start.5 = (f32[2,8]{1,0:T(2,128)S(1)}, f32[2,8]{1,0:T(2,128)}, u32[]{:S(2)}) copy-start(f32[2,8]{1,0:T(2,128)} %c_ref.7) | copy-start | bytes 196
  2.5 8.4 %collective-permute-start = (f32[120,128]{1,0:T(8,128)}, f32[120,128]{1,0:T(8,128)S(1)}, u32[]{:S(2)}, u32[]{:S(2)}) collective-permute-start(f32[120,128]{1,0:T(8,128)} %get-tuple-element.20), channel_id=1, source_target_pairs={{0,1},{1,0},{2,3},{3,2},{4,5},{5,4},{6,7},{7,6},{8,9},{9,8},{10,11... | collective-permute-start | bytes 184328 | tf_op jit(solution)/shard_map/ppermute | solution.py:604
  5.5 6.2 %collective-permute-start.1 = (f32[120,128]{1,0:T(8,128)}, f32[120,128]{1,0:T(8,128)S(1)}, u32[]{:S(2)}, u32[]{:S(2)}) collective-permute-start(f32[120,128]{1,0:T(8,128)} %get-tuple-element.21), channel_id=1, source_target_pairs={{0,3},{1,2},{2,1},{3,0},{4,7},{5,6},{6,5},{7,4},{8,11},{9,10},{10,... | collective-permute-start | bytes 184328 | tf_op jit(solution)/shard_map/ppermute | solution.py:604
  12.1 6.8 %collective-permute-start.2 = (f32[240,128]{1,0:T(8,128)S(1)}, f32[240,128]{1,0:T(8,128)S(1)}, u32[]{:S(2)}, u32[]{:S(2)}) collective-permute-start(f32[240,128]{1,0:T(8,128)S(1)} %pack_edges.1), channel_id=1, source_target_pairs={{0,4},{4,0},{8,12},{12,8},{16,20},{20,16},{24,28},{28,24},{1,5},{5... | collective-permute-start | bytes 368648 | tf_op jit(solution)/shard_map/ppermute | solution.py:604
  12.1 6.8 %collective-permute-start.3 = (f32[240,128]{1,0:T(8,128)S(1)}, f32[240,128]{1,0:T(8,128)S(1)}, u32[]{:S(2)}, u32[]{:S(2)}) collective-permute-start(f32[240,128]{1,0:T(8,128)S(1)} %pack_edges.1), channel_id=1, source_target_pairs={{0,28},{4,8},{8,4},{12,16},{16,12},{20,24},{24,20},{28,0},{1,29},{... | collective-permute-start | bytes 368648 | tf_op jit(solution)/shard_map/ppermute | solution.py:604

commit v4 on v3

--- a/solution.py
+++ b/solution.py
@@ -129,9 +129,17 @@
         north_ref[pl.ds(start, 8), :] = jnp.where(lat == last, 0.0, jnp.where(even, a, b))
 
 
-def pack_interior_kernel(c_ref, adj_ref, zon_ref, mer_ref, depth_ref, diag_ref, o_ref, own_ref, late_ref, m_ref, f_ref):
-    del c_ref
+def pack_interior_kernel(
+    c_ref, adj_ref, zon_ref, mer_ref, depth_ref, diag_ref, o_ref, own_ref, late_ref, m_ref, f_ref, factor_ref
+):
     lane = lane_iota()
+    for level in range(16):
+        factor_ref[level] = jnp.full((8, LANES), c_ref[level // 8, level % 8], jnp.float32)
+    for tracer in range(2):
+        by_group = jnp.zeros((8, LANES), jnp.float32)
+        for k in range(8):
+            by_group = jnp.where(lane // 16 == k, c_ref[tracer, k], by_group)
+        factor_ref[16 + tracer] = by_group
 
     def rows(r, carry):
         at = aligned(8 * r)
@@ -239,7 +247,7 @@
     ):
         del own_in_ref, m_in_ref, f_in_ref
         lane = lane_iota()
-        coup = [c_ref[level // 8, level % 8] for level in range(16)]
+        coup = [c_ref[level] for level in range(16)]
         square = [coup[k] * coup[k] + coup[k + 8] * coup[k + 8] for k in range(8)]
         sort_rows(ra_ref, rb_ref, south_ref, north_ref, last)
         lo, hi, mid = HALO, EXT, 2 * HALO
@@ -347,22 +355,14 @@
     return kernel
 
 
-def group_factors(c_ref, lane):
-    first = second = jnp.zeros((8, LANES), jnp.float32)
-    for k in range(8):
-        first = jnp.where(lane // 16 == k, c_ref[0, k], first)
-        second = jnp.where(lane // 16 == k, c_ref[1, k], second)
-    return first, second
-
-
 def make_sides_kernel(last, devices):
     def kernel(
-        c_ref, own_ref, pa_ref, pb_ref, block_sums_ref, shift_ref, z_ref, s_ref, sums_ref, m_ref, f_ref, all_ref
+        c_ref, own_ref, pb_ref, pa_ref, block_sums_ref, shift_ref, z_ref, s_ref, sums_ref, m_ref, f_ref, all_ref
     ):
         lane = lane_iota()
         pos = lane % 16
         level_of = (lane // 16).astype(jnp.float32)
-        first, second = group_factors(c_ref, lane)
+        first, second = c_ref[16], c_ref[17]
         square = first * first + second * second
         even_lon = lax.rem(lax.axis_index("lon"), 2) == 0
         shift = shift_ref[...]
@@ -490,8 +490,8 @@
         lane = lane_iota()
         pos = lane % 16
         level_of = (lane // 16).astype(jnp.float32)
-        coup = [c_ref[level // 8, level % 8] for level in range(16)]
-        first, second = group_factors(c_ref, lane)
+        coup = [c_ref[level] for level in range(16)]
+        first, second = c_ref[16], c_ref[17]
 
         devices = sums_ref.shape[0]
         blocks = []
@@ -622,13 +622,13 @@
             name="row_messages",
         )(*block_args)
         recv_a, recv_b = swap("lat", msg_a, msg_b)
-        packed, own, late, masked, flows = pl.pallas_call(
+        packed, own, late, masked, flows, factors = pl.pallas_call(
             pack_interior_kernel,
             in_specs=[smem] + [VMEM] * 5,
-            out_specs=[VMEM] * 5,
+            out_specs=[VMEM] * 6,
             out_shape=[
                 array(3 * EXT, LANES), array(6, EXT, LANES), array(2, ROWS, LANES),
-                array(16, PAD, LANES), array(16, PAD, LANES),
+                array(16, PAD, LANES), array(16, PAD, LANES), array(18, 8, LANES),
             ],
             compiler_params=params,
             cost_estimate=pl.CostEstimate(flops=4_000_000, bytes_accessed=1_000_000, transcendentals=0),
@@ -648,7 +648,7 @@
         side_a, side_b = swap("lon", packed, packed)
         am, pq, block, block_sums, shift, own, _, _ = pl.pallas_call(
             make_block_kernel(lat - 1),
-            in_specs=[smem] + [VMEM] * 7,
+            in_specs=[VMEM] * 8,
             out_specs=[VMEM] * 8,
             out_shape=[
                 array(16, EXT, LANES), array(16, EXT, LANES), array(10, PAD, LANES),
@@ -660,10 +660,10 @@
             compiler_params=params,
             cost_estimate=pl.CostEstimate(flops=16_000_000, bytes_accessed=4_000_000, transcendentals=0),
             name="block",
-        )(coupling, depth, surface_diag, recv_a, recv_b, own, masked, flows)
+        )(factors, depth, surface_diag, recv_a, recv_b, own, masked, flows)
         z, sides, sums = pl.pallas_call(
             make_sides_kernel(lat - 1, devices),
-            in_specs=[smem] + [VMEM] * 5,
+            in_specs=[VMEM] * 6,
             out_specs=[VMEM] * 3,
             out_shape=[array(2, 4, EXT, LANES), array(2, 10, PAD, LANES), array(devices, LANES)],
             scratch_shapes=[
@@ -673,11 +673,11 @@
             ],
             compiler_params=params,
             name="sides",
-        )(coupling, own, side_a, side_b, block_sums, shift)
+        )(factors, own, side_b, side_a, block_sums, shift)
         everyone = lax.all_to_all(sums, ("lon", "lat"), 0, 0, tiled=True)
         out, sens = pl.pallas_call(
             make_finish_kernel(lat),
-            in_specs=[smem] + [VMEM] * 9,
+            in_specs=[VMEM] * 10,
             out_specs=[VMEM] * 2,
             out_shape=[array(16, ROWS, LANES), array(ROWS, LANES)],
             scratch_shapes=[
@@ -687,7 +687,7 @@
             ],
             compiler_params=params,
             name="finish",
-        )(coupling, zonal_flow, meridional_flow, am, pq, block, late, z, sides, everyone)
+        )(factors, zonal_flow, meridional_flow, am, pq, block, late, z, sides, everyone)
         return out.reshape(adj_tracer.shape), sens
 
     return on_device

time: 35.7 us -> 34 us (0.952)
  Pallas kernels: 15.5 us -> 13.8 us
  waiting for transfers between devices: 0.89 us -> 2.05 us
  starting transfers between devices: 8.16 us -> 7.21 us
    pallas_call x3, Pallas kernels: 10.6 us -> 8.93 us  [the longest x1 3.64 us: on_device(): pl.pallas_call(make_block_kernel(lat - 1), in_specs=[VMEM] * 8, out_specs...]
    ppermute x4, waiting for transfers between devices: 0.89 us -> 2.05 us  [swap(): return (lax.ppermute(a, axis, first), lax.ppermute(b, axis, second))]
    ppermute x4, starting transfers between devices: 8.16 us -> 7.21 us  [swap(): return (lax.ppermute(a, axis, first), lax.ppermute(b, axis, second))]
  transfers between devices with their start and end apart: 4 -> 4, of which waited for: 1 -> 2; matrix products, arithmetic and copies ran while one was open for 0% -> 0% of each run, Pallas kernels for 20% -> 19%
where the time goes in v4:
time: 34 us; the launch traced here: 33.8 us
  Pallas kernels  13.8 us (41%)
  blocking collectives  9.99 us (29%)
  starting transfers between devices  7.21 us (21%)
  waiting for transfers between devices  2.05 us (6%)
  between operations  0.72 us (2%)
    all_to_all x1, blocking collectives, on_device(): everyone = lax.all_to_all(sums, ('lon', 'lat'), 0, 0, tiled=True)  9.99 us
    ppermute x4, starting transfers between devices, swap(): return (lax.ppermute(a, axis, first), lax.ppermute(b, axis, second))  7.21 us
    pallas_call x1, Pallas kernels, on_device(): pl.pallas_call(make_block_kernel(lat - 1), in_specs=[VMEM] * 8, out_specs...  3.64 us
    pallas_call x1, Pallas kernels, on_device(): pl.pallas_call(make_finish_kernel(lat), in_specs=[VMEM] * 10, out_specs=[...  2.85 us
    pallas_call x1, Pallas kernels, on_device(): pl.pallas_call(pack_interior_kernel, in_specs=[smem] + [VMEM] * 5, out_sp...  2.84 us
    pallas_call x1, Pallas kernels, on_device(): pl.pallas_call(make_sides_kernel(lat - 1, devices), in_specs=[VMEM] * 6,...  2.43 us
    ppermute x4, waiting for transfers between devices, swap(): return (lax.ppermute(a, axis, first), lax.ppermute(b, axis, second))  2.05 us
    pallas_call x1, Pallas kernels, on_device(): pl.pallas_call(row_message_kernel, in_specs=[HBM] * 5, out_specs=[VMEM] *...  1.76 us
  transfers between devices with their start and end apart: 4, of which 2 were waited for; matrix products, arithmetic and copies ran while one was open for 0% of the time, Pallas kernels for 19%

profile of v4, /device:TPU:0, one launch (start us, length us, event | category | flops | bytes accessed | tf_op | source)
XLA Modules:
  0.0 33.8 jit_solution(13777718637741764222)
XLA Ops:
  0.6 0.0 copy-start
  0.6 0.0 copy-start.1
  0.7 0.0 copy-start.2
  0.7 0.0 copy-start.3
  0.7 0.0 copy-start.4
  0.7 1.8 %row_messages.1 = (f32[120,128]{1,0:T(8,128)}, f32[120,128]{1,0:T(8,128)}) custom-call(f32[16,64,128]{2,1,0:T(8,128)} %bitcast.6, bf16[2,8,64,128]{3,2,1,0:T(8,128)(2,1)} %zon_ref.3, bf16[2,8,64,128]{3,2,1,0:T(8,128)(2,1)} %mer_ref.3, s32[64,128]{1,0:T(8,128)} %depth_ref.3, f32[64,128]{1,0:T(8,128)} %diag_ref.3), custom_call_target="tpu_custom_call" | custom-call | tf_op jit(solution)/shard_map/row_messages/pallas_call | solution.py:609
  2.4 0.0 copy-start.5
  2.5 3.1 %collective-permute-start = (f32[120,128]{1,0:T(8,128)}, f32[120,128]{1,0:T(8,128)S(1)}, u32[]{:S(2)}, u32[]{:S(2)}) collective-permute-start(f32[120,128]{1,0:T(8,128)} %get-tuple-element.22), channel_id=1, source_target_pairs={{0,1},{1,0},{2,3},{3,2},{4,5},{5,4},{6,7},{7,6},{8,9},{9,8},{10,11... | collective-permute-start | bytes 184328 | tf_op jit(solution)/shard_map/ppermute | solution.py:604
  5.5 2.5 %collective-permute-start.1 = (f32[120,128]{1,0:T(8,128)}, f32[120,128]{1,0:T(8,128)S(1)}, u32[]{:S(2)}, u32[]{:S(2)}) collective-permute-start(f32[120,128]{1,0:T(8,128)} %get-tuple-element.23), channel_id=1, source_target_pairs={{0,3},{1,2},{2,1},{3,0},{4,7},{5,6},{6,5},{7,4},{8,11},{9,10},{10,... | collective-permute-start | bytes 184328 | tf_op jit(solution)/shard_map/ppermute | solution.py:604
  8.0 0.0 copy-done
  8.0 0.0 copy-done.4
  8.0 0.0 copy-done.5
  8.1 2.8 %pack_interior.1 = (f32[240,128]{1,0:T(8,128)S(1)}, f32[6,80,128]{2,1,0:T(8,128)S(1)}, f32[2,64,128]{2,1,0:T(8,128)S(1)}, f32[16,96,128]{2,1,0:T(8,128)S(1)}, f3...) custom-call(f32[2,8]{1,0:T(2,128)S(1)} %copy-done.5, f32[16,64,128]{2,1,0:T(8,128)S(1)} %bitcast.7, ...), custom_call_target="tpu_custom_call" | custom-call | flops 4000000 | bytes 1000000 | tf_op jit(solution)/shard_map/pack_interior/pallas_call | solution.py:625
  10.9 0.0 collective-permute-done.ra_ref
  10.9 0.9 %collective-permute-done.1.rb_ref = f32[120,128]{1,0:T(8,128)S(1)} collective-permute-done((f32[120,128]{1,0:T(8,128)}, f32[120,128]{1,0:T(8,128)S(1)}, u32[]{:S(2)}, u32[]{:S(2)}) %collective-permute-start.1) | collective-permute-done | bytes 61472 | tf_op jit(solution)/shard_map/ppermute | solution.py:604
  11.8 0.3 pack_edges.1
  12.1 1.1 %collective-permute-start.2 = (f32[240,128]{1,0:T(8,128)S(1)}, f32[240,128]{1,0:T(8,128)S(1)}, u32[]{:S(2)}, u32[]{:S(2)}) collective-permute-start(f32[240,128]{1,0:T(8,128)S(1)} %pack_edges.1), channel_id=1, source_target_pairs={{0,28},{4,8},{8,4},{12,16},{16,12},{20,24},{24,20},{28,0},{1,29},{... | collective-permute-start | bytes 368648 | tf_op jit(solution)/shard_map/ppermute | solution.py:604
  13.2 0.6 %collective-permute-start.3 = (f32[240,128]{1,0:T(8,128)S(1)}, f32[240,128]{1,0:T(8,128)S(1)}, u32[]{:S(2)}, u32[]{:S(2)}) collective-permute-start(f32[240,128]{1,0:T(8,128)S(1)} %pack_edges.1), channel_id=1, source_target_pairs={{0,4},{4,0},{8,12},{12,8},{16,20},{20,16},{24,28},{28,24},{1,5},{5... | collective-permute-start | bytes 368648 | tf_op jit(solution)/shard_map/ppermute | solution.py:604
  13.7 3.6 %block.1 = (f32[16,80,128]{2,1,0:T(8,128)S(1)}, f32[16,80,128]{2,1,0:T(8,128)S(1)}, f32[10,96,128]{2,1,0:T(8,128)S(1)}, f32[280,128]{1,0:T(8,128)S(1)}, f32[8,12...) custom-call(f32[18,8,128]{2,1,0:T(8,128)S(1)} %get-tuple-element.21., ...), custom_call_target="tpu_custom_call", output_to_operand_aliasing={{5}: (5, {}), {6}: (6, {}), {7}: (7, {})} | custom-call | flops 16000000 | bytes 4000000 | tf_op jit(solution)/shard_map/block/pallas_call | solution.py:649
  17.4 1.2 %collective-permute-done.2.pb_ref = f32[240,128]{1,0:T(8,128)S(1)} collective-permute-done((f32[240,128]{1,0:T(8,128)S(1)}, f32[240,128]{1,0:T(8,128)S(1)}, u32[]{:S(2)}, u32[]{:S(2)}) %collective-permute-start.2) | collective-permute-done | bytes 122912 | tf_op jit(solution)/shard_map/ppermute | solution.py:604
  18.5 0.0 collective-permute-done.3.pa_ref
  18.5 2.4 %sides.1 = (f32[2,4,80,128]{3,2,1,0:T(8,128)S(1)}, f32[2,10,96,128]{3,2,1,0:T(8,128)S(1)}, f32[32,128]{1,0:T(8,128)S(1)}) custom-call(f32[18,8,128]{2,1,0:T(8,128)S(1)} %get-tuple-element.21.c_ref, f32[6,80,128]{2,1,0:T(8,128)S(1)} %get-tuple-element.31.own_ref, f32[240,128]{1,0:T(8,128)S(1)} %collective-permute-done.2.pb_ref, ...), custom_call_target="tpu_custom_call" | custom-call | tf_op jit(solution)/shard_map/sides/pallas_call | solution.py:664
  21.0 10.0 %all_to_all.11 = f32[32,1,128]{2,1,0:T(1,128)S(1)} all-to-all(f32[32,1,128]{2,1,0:T(1,128)S(1)} %bitcast.9), channel_id=1, replica_groups=mesh['lon'=8,'lat'=4] {'lon','lat'}, dimensions={0} | all-to-all | bytes 32768 | tf_op jit(solution)/shard_map/all_to_all | solution.py:677
  31.0 2.9 %finish.1 = (f32[16,64,128]{2,1,0:T(8,128)}, f32[64,128]{1,0:T(8,128)}) custom-call(f32[18,8,128]{2,1,0:T(8,128)S(1)} %get-tuple-element.21.c_ref, bf16[2,8,64,128]{3,2,1,0:T(8,128)(2,1)S(1)} %copy-done, bf16[2,8,64,128]{3,2,1,0:T(8,128)(2,1)S(1)} %copy-done.1, f32[16,80,128]{2,1,0:T(8,128)S(1)} %get-tuple-element.27.am_ref, ...), custom_call_target="tpu_custom_call" | custom-call | tf_op jit(solution)/shard_map/finish/pallas_call | solution.py:678
  (3 shorter events, 0.0 us)
Async XLA Ops:
  0.6 7.4 %copy-start = (bf16[2,8,64,128]{3,2,1,0:T(8,128)(2,1)S(1)}, bf16[2,8,64,128]{3,2,1,0:T(8,128)(2,1)}, u32[]{:S(2)}) copy-start(bf16[2,8,64,128]{3,2,1,0:T(8,128)(2,1)} %zon_ref.3) | copy-start | bytes 786436
  0.6 7.4 %copy-start.1 = (bf16[2,8,64,128]{3,2,1,0:T(8,128)(2,1)S(1)}, bf16[2,8,64,128]{3,2,1,0:T(8,128)(2,1)}, u32[]{:S(2)}) copy-start(bf16[2,8,64,128]{3,2,1,0:T(8,128)(2,1)} %mer_ref.3) | copy-start | bytes 786436
  0.7 7.4 %copy-start.2 = (f32[2,8,64,128]{3,2,1,0:T(8,128)S(1)}, f32[2,8,64,128]{3,2,1,0:T(8,128)}, u32[]{:S(2)}) copy-start(f32[2,8,64,128]{3,2,1,0:T(8,128)} %param.6) | copy-start | bytes 1572868
  0.7 7.4 %copy-start.3 = (s32[64,128]{1,0:T(8,128)S(1)}, s32[64,128]{1,0:T(8,128)}, u32[]{:S(2)}) copy-start(s32[64,128]{1,0:T(8,128)} %depth_ref.3) | copy-start | bytes 98308
  0.7 7.4 %copy-start.4 = (f32[64,128]{1,0:T(8,128)S(1)}, f32[64,128]{1,0:T(8,128)}, u32[]{:S(2)}) copy-start(f32[64,128]{1,0:T(8,128)} %diag_ref.3) | copy-start | bytes 98308
  2.4 5.6 %copy-start.5 = (f32[2,8]{1,0:T(2,128)S(1)}, f32[2,8]{1,0:T(2,128)}, u32[]{:S(2)}) copy-start(f32[2,8]{1,0:T(2,128)} %c_ref.1) | copy-start | bytes 196
  2.5 8.4 %collective-permute-start = (f32[120,128]{1,0:T(8,128)}, f32[120,128]{1,0:T(8,128)S(1)}, u32[]{:S(2)}, u32[]{:S(2)}) collective-permute-start(f32[120,128]{1,0:T(8,128)} %get-tuple-element.22), channel_id=1, source_target_pairs={{0,1},{1,0},{2,3},{3,2},{4,5},{5,4},{6,7},{7,6},{8,9},{9,8},{10,11... | collective-permute-start | bytes 184328 | tf_op jit(solution)/shard_map/ppermute | solution.py:604
  5.5 6.2 %collective-permute-start.1 = (f32[120,128]{1,0:T(8,128)}, f32[120,128]{1,0:T(8,128)S(1)}, u32[]{:S(2)}, u32[]{:S(2)}) collective-permute-start(f32[120,128]{1,0:T(8,128)} %get-tuple-element.23), channel_id=1, source_target_pairs={{0,3},{1,2},{2,1},{3,0},{4,7},{5,6},{6,5},{7,4},{8,11},{9,10},{10,... | collective-permute-start | bytes 184328 | tf_op jit(solution)/shard_map/ppermute | solution.py:604
  12.1 6.5 %collective-permute-start.2 = (f32[240,128]{1,0:T(8,128)S(1)}, f32[240,128]{1,0:T(8,128)S(1)}, u32[]{:S(2)}, u32[]{:S(2)}) collective-permute-start(f32[240,128]{1,0:T(8,128)S(1)} %pack_edges.1), channel_id=1, source_target_pairs={{0,28},{4,8},{8,4},{12,16},{16,12},{20,24},{24,20},{28,0},{1,29},{... | collective-permute-start | bytes 368648 | tf_op jit(solution)/shard_map/ppermute | solution.py:604
  13.2 5.4 %collective-permute-start.3 = (f32[240,128]{1,0:T(8,128)S(1)}, f32[240,128]{1,0:T(8,128)S(1)}, u32[]{:S(2)}, u32[]{:S(2)}) collective-permute-start(f32[240,128]{1,0:T(8,128)S(1)} %pack_edges.1), channel_id=1, source_target_pairs={{0,4},{4,0},{8,12},{12,8},{16,20},{20,16},{24,28},{28,24},{1,5},{5... | collective-permute-start | bytes 368648 | tf_op jit(solution)/shard_map/ppermute | solution.py:604

commit v5 on v4

--- a/solution.py
+++ b/solution.py
@@ -16,6 +16,7 @@
 FLOW_AT, MASK_AT, DEPTH_AT, DIAG_AT, MSG_ROWS = 8, 40, 104, 108, 120
 DEP, DIA, B, H, U, V, W, HU, HV, HW = range(10)
 M0, M1, FU, FV, PDEP, PDIA = range(6)
+SIDE_ROWS = EXT + 8
 FIRST, LAST = 4, LANES - 5
 PAIRS = ((0, 0), (0, 1), (0, 2), (1, 1), (1, 2), (2, 2))
 NSUMS = 5 + 5 * len(PAIRS)
@@ -41,21 +42,8 @@
     return over_groups(jnp.where(lane < 16, x, 0.0))
 
 
-def message_shift(level):
-    return 16 * (level % 8) + 8 * (level // 8) + 4
-
-
 def own_shift(level):
     return 16 * (level % 8) + 8
-
-
-def pack_messages(values, lane):
-    eighth = lane // 8
-    packed = values[0]
-    for level, value in enumerate(values):
-        turned = roll(value, message_shift(level))
-        packed = jnp.where(eighth == 2 * (level % 8) + level // 8, turned, packed) if level else turned
-    return packed
 
 
 def pack_own(values, lane):
@@ -65,8 +53,23 @@
     return packed
 
 
-def pack_surface(depth, diag, lane):
-    return in_every_group(jnp.where(lane % 16 < 8, roll(depth, 4), roll(diag, 12)), lane)
+def side_messages(own, surface, lane):
+    pos = lane % 16
+    third = pos // 4
+
+    def merge(parts):
+        value = parts[0]
+        for index in range(1, 4):
+            value = jnp.where(third == index, parts[index], value)
+        return value
+
+    to_east = merge([roll(own[0], -4), own[1], roll(own[2], 4), roll(own[3], 8)])
+    to_west = merge([roll(own[0], -8), roll(own[1], -4), own[2], roll(own[3], 4)])
+    depth, diag = surface
+    east = jnp.where(pos < 4, roll(depth, -4), diag)
+    west = jnp.where(pos < 4, roll(depth, -8), roll(diag, -4))
+    east, west = [jnp.where(pos < 8, v, roll(v, 8)) for v in (east, west)]
+    return to_east, to_west, east, west
 
 
 def aligned(start, count=8):
@@ -130,11 +133,14 @@
 
 
 def pack_interior_kernel(
-    c_ref, adj_ref, zon_ref, mer_ref, depth_ref, diag_ref, o_ref, own_ref, late_ref, m_ref, f_ref, factor_ref
+    c_ref, adj_ref, zon_ref, mer_ref, depth_ref, diag_ref,
+    a_ref, b_ref, own_ref, late_ref, m_ref, f_ref, s_ref, factor_ref,
 ):
     lane = lane_iota()
+    even = lax.rem(lax.axis_index("lon"), 2) == 0
+    coup = [jnp.full((8, LANES), c_ref[level // 8, level % 8], jnp.float32) for level in range(16)]
     for level in range(16):
-        factor_ref[level] = jnp.full((8, LANES), c_ref[level // 8, level % 8], jnp.float32)
+        factor_ref[level] = coup[level]
     for tracer in range(2):
         by_group = jnp.zeros((8, LANES), jnp.float32)
         for k in range(8):
@@ -144,44 +150,63 @@
     def rows(r, carry):
         at = aligned(8 * r)
         to = aligned(8 * r + HALO)
+        far = aligned(8 * r + 2 * HALO)
         depth = depth_ref[at, :].astype(jnp.float32)
         diag = diag_ref[at, :]
+        s_ref[DEP, far, :] = depth
+        s_ref[DIA, far, :] = diag
         masked = [jnp.where(depth > float(level % 8), adj_ref[level, at, :], 0.0) for level in range(16)]
         flows = [
             0.5 * ref[1, k, at, :].astype(jnp.float32) for ref in (zon_ref, mer_ref) for k in range(8)
         ]
         for level in range(16):
-            m_ref[level, aligned(8 * r + 2 * HALO), :] = masked[level]
-            f_ref[level, aligned(8 * r + 2 * HALO), :] = flows[level]
-        o_ref[to, :] = pack_messages(masked, lane)
-        o_ref[aligned(EXT + 8 * r + HALO), :] = pack_messages(flows, lane)
-        o_ref[aligned(2 * EXT + 8 * r + HALO), :] = pack_surface(depth, diag, lane)
-        own_ref[M0, to, :] = pack_own(masked[:8], lane)
-        own_ref[M1, to, :] = pack_own(masked[8:], lane)
-        own_ref[FU, to, :] = pack_own(flows[:8], lane)
-        own_ref[FV, to, :] = pack_own(flows[8:], lane)
-        own_ref[PDEP, to, :] = in_every_group(roll(depth, 8), lane)
-        own_ref[PDIA, to, :] = in_every_group(roll(diag, 8), lane)
+            m_ref[level, far, :] = masked[level]
+            f_ref[level, far, :] = flows[level]
+        parts = [factor_ref[level] * masked[level] for level in range(16)]
+        while len(parts) > 1:
+            parts = [parts[i] + parts[i + 1] for i in range(0, len(parts), 2)]
+        s_ref[B, far, :] = parts[0]
+        own = [pack_own(v, lane) for v in (masked[:8], masked[8:], flows[:8], flows[8:])]
+        surface = [in_every_group(roll(v, 8), lane) for v in (depth, diag)]
+        for slot, value in enumerate(own + surface):
+            own_ref[slot, to, :] = value
+        to_east, to_west, east, west = side_messages(own, surface, lane)
+        a_ref[to, :] = jnp.where(even, to_east, to_west)
+        b_ref[to, :] = jnp.where(even, to_west, to_east)
+        here = lane // 8 == r + 1
         for which, ref in enumerate((zon_ref, mer_ref)):
             late_ref[which, at, :] = pack_own([0.5 * ref[0, k, at, :].astype(jnp.float32) for k in range(8)], lane)
-        return carry
-
-    lax.fori_loop(0, ROWS // 8, rows, 0)
+        return jnp.where(here, east, carry[0]), jnp.where(here, west, carry[1])
+
+    zero = jnp.zeros((8, LANES), jnp.float32)
+    east, west = lax.fori_loop(0, ROWS // 8, rows, (zero, zero), unroll=2)
+    a_ref[EXT : EXT + 8, :] = jnp.where(even, east, west)
+    b_ref[EXT : EXT + 8, :] = jnp.where(even, west, east)
 
 
 def make_pack_edges_kernel(last):
-    def kernel(ra_ref, rb_ref, o_in_ref, o_ref, south_ref, north_ref):
-        del o_in_ref
+    def kernel(ra_ref, rb_ref, a_in_ref, b_in_ref, own_in_ref, a_ref, b_ref, own_ref, south_ref, north_ref):
+        del own_in_ref
         sort_rows(ra_ref, rb_ref, south_ref, north_ref, last)
         lane = lane_iota()
+        even = lax.rem(lax.axis_index("lon"), 2) == 0
+        surface_a, surface_b = [ref[EXT : EXT + 8, :] for ref in (a_in_ref, b_in_ref)]
         for ref, south, base in ((south_ref, True, 0), (north_ref, False, HALO + ROWS)):
+            rows = pl.ds(base, 8)
             masked = [level_rows(ref, MASK_AT, 4, level, south) for level in range(16)]
-            o_ref[base : base + 8, :] = pack_messages(masked, lane)
             flows = [level_rows(ref, FLOW_AT, 2, level, south) for level in range(16)]
-            o_ref[EXT + base : EXT + base + 8, :] = pack_messages(flows, lane)
-            depth = level_rows(ref, DEPTH_AT, 4, 0, south)
-            diag = level_rows(ref, DIAG_AT, 4, 0, south)
-            o_ref[2 * EXT + base : 2 * EXT + base + 8, :] = pack_surface(depth, diag, lane)
+            own = [pack_own(v, lane) for v in (masked[:8], masked[8:], flows[:8], flows[8:])]
+            surface = [in_every_group(roll(level_rows(ref, at, 4, 0, south), 8), lane) for at in (DEPTH_AT, DIAG_AT)]
+            for slot, value in enumerate(own + surface):
+                own_ref[slot, rows, :] = value
+            to_east, to_west, east, west = side_messages(own, surface, lane)
+            a_ref[rows, :] = jnp.where(even, to_east, to_west)
+            b_ref[rows, :] = jnp.where(even, to_west, to_east)
+            here = lane // 8 == base // 8
+            surface_a = jnp.where(here, jnp.where(even, east, west), surface_a)
+            surface_b = jnp.where(here, jnp.where(even, west, east), surface_b)
+        a_ref[EXT : EXT + 8, :] = surface_a
+        b_ref[EXT : EXT + 8, :] = surface_b
 
     return kernel
 
@@ -241,16 +266,16 @@
 
 def make_block_kernel(last):
     def kernel(
-        c_ref, depth_ref, diag_ref, ra_ref, rb_ref, own_in_ref, m_in_ref, f_in_ref,
-        am_ref, pq_ref, s_ref, sums_ref, shift_ref, own_ref, m_ref, f_ref,
+        c_ref, ra_ref, rb_ref, m_in_ref, f_in_ref, s_in_ref,
+        am_ref, pq_ref, sums_ref, shift_ref, m_ref, f_ref, s_ref,
         south_ref, north_ref,
     ):
-        del own_in_ref, m_in_ref, f_in_ref
+        del m_in_ref, f_in_ref, s_in_ref
         lane = lane_iota()
         coup = [c_ref[level] for level in range(16)]
         square = [coup[k] * coup[k] + coup[k + 8] * coup[k + 8] for k in range(8)]
         sort_rows(ra_ref, rb_ref, south_ref, north_ref, last)
-        lo, hi, mid = HALO, EXT, 2 * HALO
+        lo, hi = HALO, EXT
         for level in range(16):
             for ref, at, count in ((m_ref, MASK_AT, 4), (f_ref, FLOW_AT, 2)):
                 ref[level, lo : lo + 8, :] = level_rows(south_ref, at, count, level, True)
@@ -259,18 +284,12 @@
             s_ref[field, lo : lo + 8, :] = level_rows(south_ref, at, 4, 0, True)
             s_ref[field, hi : hi + 8, :] = level_rows(north_ref, at, 4, 0, False)
 
-        s_ref[DEP, mid : mid + ROWS, :] = depth_ref[...].astype(jnp.float32)
-        s_ref[DIA, mid : mid + ROWS, :] = diag_ref[...]
-
-        def rhs(r, carry):
+        for r in (0, CHUNKS - 1):
             at = rows_at(r)
             parts = [coup[level] * m_ref[level, at, :] for level in range(16)]
             while len(parts) > 1:
                 parts = [parts[i] + parts[i + 1] for i in range(0, len(parts), 2)]
             s_ref[B, at, :] = parts[0]
-            return carry
-
-        lax.fori_loop(0, CHUNKS, rhs, 0)
 
         zero = jnp.zeros((8, LANES), jnp.float32)
 
@@ -278,7 +297,7 @@
             b = s_ref[B, rows_at(r), :]
             return carry[0] + b * b, carry[1] + b * shifted(s_ref.at[B], s_ref.at[DIA], r)
 
-        squares, images_sum = lax.fori_loop(1, CHUNKS - 1, quotient, (zero, zero), unroll=2)
+        squares, images_sum = lax.fori_loop(1, CHUNKS - 1, quotient, (zero, zero), unroll=8)
         inside = (lane > 0) & (lane < LANES - 1)
         squares, images_sum = [
             jnp.sum(jnp.sum(jnp.where(inside, v, 0.0), axis=0, keepdims=True), axis=1, keepdims=True)
@@ -293,7 +312,7 @@
             s_ref[H, rows_at(r), :] = on_grid(r, last, shifted(s_ref.at[B], s_ref.at[DIA], r))
             return carry
 
-        lax.fori_loop(0, CHUNKS, images, 0, unroll=2)
+        lax.fori_loop(0, CHUNKS, images, 0, unroll=10)
 
         def advect(r, carry):
             out_at = aligned(8 * r)
@@ -330,7 +349,7 @@
                 s_ref[target, rows_at(r), :] = on_grid(r, last, shifted(s_ref.at[source], s_ref.at[DIA], r))
             return carry
 
-        lax.fori_loop(0, CHUNKS, images_two, 0, unroll=2)
+        lax.fori_loop(0, CHUNKS, images_two, 0, unroll=5)
 
         def gather(r, sums):
             at = rows_at(r)
@@ -338,19 +357,10 @@
             b, h, *rest = [s_ref[field, at, :] for field in (B, H, U, V, W, HU, HV, HW)]
             return tuple(s + n for s, n in zip(sums, products(b, h, hh, rest[:3], rest[3:], second)))
 
-        sums = lax.fori_loop(1, CHUNKS - 1, gather, (zero,) * NSUMS)
+        sums = lax.fori_loop(1, CHUNKS - 1, gather, (zero,) * NSUMS, unroll=2)
         keep = (lane >= FIRST) & (lane <= LAST)
         for index, value in enumerate(sums):
             sums_ref[8 * index : 8 * index + 8, :] = jnp.where(keep, value, 0.0)
-
-        for ref, south, base in ((south_ref, True, 0), (north_ref, False, HALO + ROWS)):
-            rows = pl.ds(base, 8)
-            for slot, at, count in ((M0, MASK_AT, 4), (FU, FLOW_AT, 2)):
-                values = [level_rows(ref, at, count, level, south) for level in range(16)]
-                own_ref[slot, rows, :] = pack_own(values[:8], lane)
-                own_ref[slot + 1, rows, :] = pack_own(values[8:], lane)
-            for slot, at in ((PDEP, DEPTH_AT), (PDIA, DIAG_AT)):
-                own_ref[slot, rows, :] = in_every_group(roll(level_rows(ref, at, 4, 0, south), 8), lane)
 
     return kernel
 
@@ -367,30 +377,30 @@
         even_lon = lax.rem(lax.axis_index("lon"), 2) == 0
         shift = shift_ref[...]
 
-        def assemble(r, carry):
-            at = rows_at(r)
-            own_at = aligned(8 * r)
+        a_last, b_last = pa_ref[EXT : EXT + 8, :], pb_ref[EXT : EXT + 8, :]
+        surfaces = (jnp.where(even_lon, a_last, b_last), jnp.where(even_lon, b_last, a_last))
+
+        def assemble(r):
+            at, rows = pl.ds(8 * r + HALO, 8), pl.ds(8 * r, 8)
             for side in range(2):
                 outer = pos >= 8 if side == 0 else pos < 8
-                for part in range(3):
-                    src = aligned(part * EXT + 8 * r)
-                    a, b = pa_ref[src, :], pb_ref[src, :]
-                    got = jnp.where(even_lon, a, b) if side == 0 else jnp.where(even_lon, b, a)
-                    one = jnp.where(outer, roll(got, 4), own_ref[2 * part, own_at, :])
-                    two = jnp.where(outer, roll(got, -4), own_ref[2 * part + 1, own_at, :])
-                    if part == 0:
-                        m_ref[side, 0, at, :] = one
-                        m_ref[side, 1, at, :] = two
-                        s_ref[side, B, at, :] = over_groups(first * one + second * two)
-                    elif part == 1:
-                        f_ref[side, 0, at, :] = one
-                        f_ref[side, 1, at, :] = two
-                    else:
-                        s_ref[side, DEP, at, :] = one
-                        s_ref[side, DIA, at, :] = two - shift
-            return carry
-
-        lax.fori_loop(0, CHUNKS, assemble, 0, unroll=10)
+                a, b = pa_ref[rows, :], pb_ref[rows, :]
+                got = jnp.where(even_lon, a, b) if side == 0 else jnp.where(even_lon, b, a)
+                by = 8 if side == 0 else 4
+                one, two, u, w = [
+                    jnp.where(outer, roll(got, by - 4 * slot), own_ref[slot, rows, :]) for slot in range(4)
+                ]
+                m_ref[side, 0, at, :] = one
+                m_ref[side, 1, at, :] = two
+                s_ref[side, B, at, :] = over_groups(first * one + second * two)
+                f_ref[side, 0, at, :] = u
+                f_ref[side, 1, at, :] = w
+                got = over_groups(jnp.where(lane < 8, roll(surfaces[side], -8 * r), 0.0))
+                s_ref[side, DEP, at, :] = jnp.where(outer, roll(got, by), own_ref[PDEP, rows, :])
+                s_ref[side, DIA, at, :] = jnp.where(outer, roll(got, by - 4), own_ref[PDIA, rows, :]) - shift
+
+        for r in range(CHUNKS):
+            assemble(r)
 
         def images(r, carry):
             for side in range(2):
@@ -425,7 +435,7 @@
                     s_ref[side, target, rows_at(r), :] = on_grid(r, last, value)
             return carry
 
-        lax.fori_loop(0, CHUNKS, images_two, 0, unroll=5)
+        lax.fori_loop(0, CHUNKS, images_two, 0, unroll=10)
 
         east = lane < 8
 
@@ -444,7 +454,7 @@
             return tuple(s + n for s, n in zip(sums, products(b, h, hh, rest[:3], rest[3:], second_image)))
 
         zero = jnp.zeros((8, LANES), jnp.float32)
-        sums = lax.fori_loop(1, CHUNKS - 1, gather, (zero,) * NSUMS, unroll=1)
+        sums = lax.fori_loop(1, CHUNKS - 1, gather, (zero,) * NSUMS, unroll=8)
         keep = (lane >= 4) & (lane < 12)
         for index, value in enumerate(sums):
             at = pl.ds(8 * index, 8)
@@ -618,49 +628,49 @@
                 pltpu.VMEM((2, 8, LANES), f32),
                 pltpu.SemaphoreType.DMA((10,)),
             ],
-            compiler_params=pltpu.CompilerParams(vmem_limit_bytes=62914560),
+            compiler_params=pltpu.CompilerParams(vmem_limit_bytes=16*2**20),
             name="row_messages",
-        )(*block_args)
+        )(*[pltpu.with_memory_space_constraint(x, pltpu.HBM) for x in block_args])
         recv_a, recv_b = swap("lat", msg_a, msg_b)
-        packed, own, late, masked, flows, factors = pl.pallas_call(
+        shapes = [
+            (SIDE_ROWS, LANES), (SIDE_ROWS, LANES), (6, EXT, LANES), (2, ROWS, LANES),
+            (16, PAD, LANES), (16, PAD, LANES), (10, PAD, LANES), (18, 8, LANES),
+        ]
+        cols_a, cols_b, own, late, masked, flows, surface, factors = pl.pallas_call(
             pack_interior_kernel,
             in_specs=[smem] + [VMEM] * 5,
-            out_specs=[VMEM] * 6,
-            out_shape=[
-                array(3 * EXT, LANES), array(6, EXT, LANES), array(2, ROWS, LANES),
-                array(16, PAD, LANES), array(16, PAD, LANES), array(18, 8, LANES),
-            ],
+            out_specs=[VMEM] * len(shapes),
+            out_shape=[array(*shape) for shape in shapes],
             compiler_params=params,
             cost_estimate=pl.CostEstimate(flops=4_000_000, bytes_accessed=1_000_000, transcendentals=0),
             name="pack_interior",
         )(coupling, *block_args)
         row_scratch = [pltpu.VMEM((MSG_ROWS, LANES), f32)] * 2
-        packed = pl.pallas_call(
+        cols_a, cols_b, own = pl.pallas_call(
             make_pack_edges_kernel(lat - 1),
-            in_specs=[VMEM] * 3,
-            out_specs=VMEM,
-            out_shape=array(3 * EXT, LANES),
+            in_specs=[VMEM] * 5,
+            out_specs=[VMEM] * 3,
+            out_shape=[array(*shape) for shape in shapes[:3]],
             scratch_shapes=row_scratch,
-            input_output_aliases={2: 0},
+            input_output_aliases={2: 0, 3: 1, 4: 2},
             compiler_params=params,
             name="pack_edges",
-        )(recv_a, recv_b, packed)
-        side_a, side_b = swap("lon", packed, packed)
-        am, pq, block, block_sums, shift, own, _, _ = pl.pallas_call(
+        )(recv_a, recv_b, cols_a, cols_b, own)
+        side_a, side_b = swap("lon", cols_a, cols_b)
+        am, pq, block_sums, shift, _, _, block = pl.pallas_call(
             make_block_kernel(lat - 1),
-            in_specs=[VMEM] * 8,
-            out_specs=[VMEM] * 8,
+            in_specs=[VMEM] * 6,
+            out_specs=[VMEM] * 7,
             out_shape=[
-                array(16, EXT, LANES), array(16, EXT, LANES), array(10, PAD, LANES),
-                array(8 * NSUMS, LANES), array(8, LANES), array(6, EXT, LANES),
-                array(16, PAD, LANES), array(16, PAD, LANES),
+                array(16, EXT, LANES), array(16, EXT, LANES), array(8 * NSUMS, LANES), array(8, LANES),
+                array(16, PAD, LANES), array(16, PAD, LANES), array(10, PAD, LANES),
             ],
             scratch_shapes=row_scratch,
-            input_output_aliases={5: 5, 6: 6, 7: 7},
+            input_output_aliases={3: 4, 4: 5, 5: 6},
             compiler_params=params,
             cost_estimate=pl.CostEstimate(flops=16_000_000, bytes_accessed=4_000_000, transcendentals=0),
             name="block",
-        )(factors, depth, surface_diag, recv_a, recv_b, own, masked, flows)
+        )(factors, recv_a, recv_b, masked, flows, surface)
         z, sides, sums = pl.pallas_call(
             make_sides_kernel(lat - 1, devices),
             in_specs=[VMEM] * 6,

time: 34 us -> 31.4 us (0.924)
  Pallas kernels: 13.8 us -> 10.6 us
  blocking collectives: 9.99 us -> 10.4 us
    pallas_call x2, Pallas kernels: 3.93 us -> 2.49 us  [the longest x1 2.06 us: on_device(): pl.pallas_call(make_block_kernel(lat - 1), in_specs=[VMEM] * 6, out_specs...]
    pallas_call x1, Pallas kernels: 1.76 us -> 1.12 us  [on_device(): pl.pallas_call(row_message_kernel, in_specs=[HBM] * 5, out_specs=[VMEM] *...]
    pallas_call x1, Pallas kernels: 2.43 us -> 1.8 us  [on_device(): pl.pallas_call(make_sides_kernel(lat - 1, devices), in_specs=[VMEM] * 6,...]
    pallas_call x1, Pallas kernels: 2.84 us -> 2.36 us  [on_device(): pl.pallas_call(pack_interior_kernel, in_specs=[smem] + [VMEM] * 5, out_sp...]
    all_to_all x1, blocking collectives: 9.99 us -> 10.4 us  [on_device(): everyone = lax.all_to_all(sums, ('lon', 'lat'), 0, 0, tiled=True)]
  transfers between devices with their start and end apart: 4 -> 4, of which waited for: 2 -> 2; matrix products, arithmetic and copies ran while one was open for 0% -> 0% of each run, Pallas kernels for 19% -> 14%
where the time goes in v5:
time: 31.4 us; the launch traced here: 31.2 us
  Pallas kernels  10.6 us (34%)
  blocking collectives  10.4 us (33%)
  starting transfers between devices  7.21 us (23%)
  waiting for transfers between devices  2.22 us (7%)
  between operations  0.73 us (2%)
    all_to_all x1, blocking collectives, on_device(): everyone = lax.all_to_all(sums, ('lon', 'lat'), 0, 0, tiled=True)  10.4 us
    ppermute x4, starting transfers between devices, swap(): return (lax.ppermute(a, axis, first), lax.ppermute(b, axis, second))  7.21 us
    pallas_call x1, Pallas kernels, on_device(): pl.pallas_call(make_finish_kernel(lat), in_specs=[VMEM] * 10, out_specs=[...  2.86 us
    pallas_call x1, Pallas kernels, on_device(): pl.pallas_call(pack_interior_kernel, in_specs=[smem] + [VMEM] * 5, out_sp...  2.36 us
    ppermute x4, waiting for transfers between devices, swap(): return (lax.ppermute(a, axis, first), lax.ppermute(b, axis, second))  2.22 us
    pallas_call x1, Pallas kernels, on_device(): pl.pallas_call(make_block_kernel(lat - 1), in_specs=[VMEM] * 6, out_specs...  2.06 us
    pallas_call x1, Pallas kernels, on_device(): pl.pallas_call(make_sides_kernel(lat - 1, devices), in_specs=[VMEM] * 6,...  1.8 us
    pallas_call x1, Pallas kernels, on_device(): pl.pallas_call(row_message_kernel, in_specs=[HBM] * 5, out_specs=[VMEM] *...  1.12 us
  transfers between devices with their start and end apart: 4, of which 2 were waited for; matrix products, arithmetic and copies ran while one was open for 0% of the time, Pallas kernels for 14%

profile of v5, /device:TPU:0, one launch (start us, length us, event | category | flops | bytes accessed | tf_op | source)
XLA Modules:
  0.0 31.2 jit_solution(15783629454563371132)
XLA Ops:
  0.6 0.0 copy-start
  0.6 0.0 copy-start.1
  0.7 0.0 copy-start.2
  0.7 0.0 copy-start.3
  0.7 0.0 copy-start.4
  0.7 1.1 %row_messages.1 = (f32[120,128]{1,0:T(8,128)S(1)}, f32[120,128]{1,0:T(8,128)S(1)}) custom-call(f32[16,64,128]{2,1,0:T(8,128)} %bitcast.6, bf16[2,8,64,128]{3,2,1,0:T(8,128)(2,1)} %zon_ref.3, bf16[2,8,64,128]{3,2,1,0:T(8,128)(2,1)} %mer_ref.3, s32[64,128]{1,0:T(8,128)} %depth.1, f32[64,128]{1,0:T(8,128)} %diag.1), custom_call_target="tpu_custom_call" | custom-call | tf_op jit(solution)/shard_map/row_messages/pallas_call | solution.py:619
  1.8 0.0 copy-start.5
  1.8 3.1 %collective-permute-start = (f32[120,128]{1,0:T(8,128)S(1)}, f32[120,128]{1,0:T(8,128)S(1)}, u32[]{:S(2)}, u32[]{:S(2)}) collective-permute-start(f32[120,128]{1,0:T(8,128)S(1)} %get-tuple-element.26), channel_id=1, source_target_pairs={{0,1},{1,0},{2,3},{3,2},{4,5},{5,4},{6,7},{7,6},{8,9},{9,8},{10,11... | collective-permute-start | bytes 184328 | tf_op jit(solution)/shard_map/ppermute | solution.py:614
  4.9 2.5 %collective-permute-start.1 = (f32[120,128]{1,0:T(8,128)S(1)}, f32[120,128]{1,0:T(8,128)S(1)}, u32[]{:S(2)}, u32[]{:S(2)}) collective-permute-start(f32[120,128]{1,0:T(8,128)S(1)} %get-tuple-element.27), channel_id=1, source_target_pairs={{0,3},{1,2},{2,1},{3,0},{4,7},{5,6},{6,5},{7,4},{8,11},{9,10},{10,... | collective-permute-start | bytes 184328 | tf_op jit(solution)/shard_map/ppermute | solution.py:614
  7.4 0.0 copy-done
  7.4 0.0 copy-done.1
  7.4 0.0 copy-done.2
  7.4 2.4 %pack_interior.1 = (f32[88,128]{1,0:T(8,128)S(1)}, f32[88,128]{1,0:T(8,128)S(1)}, f32[6,80,128]{2,1,0:T(8,128)S(1)}, f32[2,64,128]{2,1,0:T(8,128)S(1)}, f32[16,9...) custom-call(f32[2,8]{1,0:T(2,128)S(1)} %copy-done.5, ...), custom_call_target="tpu_custom_call" | custom-call | flops 4000000 | bytes 1000000 | tf_op jit(solution)/shard_map/pack_interior/pallas_call | solution.py:639
  9.8 0.0 collective-permute-done.ra_ref
  9.8 1.1 %collective-permute-done.1.rb_ref = f32[120,128]{1,0:T(8,128)S(1)} collective-permute-done((f32[120,128]{1,0:T(8,128)S(1)}, f32[120,128]{1,0:T(8,128)S(1)}, u32[]{:S(2)}, u32[]{:S(2)}) %collective-permute-start.1) | collective-permute-done | bytes 61472 | tf_op jit(solution)/shard_map/ppermute | solution.py:614
  10.9 0.4 %pack_edges.1 = (f32[88,128]{1,0:T(8,128)S(1)}, f32[88,128]{1,0:T(8,128)S(1)}, f32[6,80,128]{2,1,0:T(8,128)S(1)}) custom-call(f32[120,128]{1,0:T(8,128)S(1)} %collective-permute-done.ra_ref, f32[120,128]{1,0:T(8,128)S(1)} %collective-permute-done.1.rb_ref, ...), custom_call_target="tpu_custom_call", output_to_operand_aliasing={{0}: (2, {}), {1}: (3, {}), {2}: (4, {})} | custom-call | tf_op jit(solution)/shard_map/pack_edges/pallas_call | solution.py:649
  11.4 1.1 %collective-permute-start.2 = (f32[88,128]{1,0:T(8,128)S(1)}, f32[88,128]{1,0:T(8,128)S(1)}, u32[]{:S(2)}, u32[]{:S(2)}) collective-permute-start(f32[88,128]{1,0:T(8,128)S(1)} %get-tuple-element.39), channel_id=1, source_target_pairs={{0,28},{4,8},{8,4},{12,16},{16,12},{20,24},{24,20},{28,0},{1,29},{... | collective-permute-start | bytes 135176 | tf_op jit(solution)/shard_map/ppermute | solution.py:614
  12.5 0.6 %collective-permute-start.3 = (f32[88,128]{1,0:T(8,128)S(1)}, f32[88,128]{1,0:T(8,128)S(1)}, u32[]{:S(2)}, u32[]{:S(2)}) collective-permute-start(f32[88,128]{1,0:T(8,128)S(1)} %get-tuple-element.40), channel_id=1, source_target_pairs={{0,4},{4,0},{8,12},{12,8},{16,20},{20,16},{24,28},{28,24},{1,5},{5... | collective-permute-start | bytes 135176 | tf_op jit(solution)/shard_map/ppermute | solution.py:614
  13.0 2.1 %block.1 = (f32[16,80,128]{2,1,0:T(8,128)S(1)}, f32[16,80,128]{2,1,0:T(8,128)S(1)}, f32[280,128]{1,0:T(8,128)S(1)}, f32[8,128]{1,0:T(8,128)S(1)}, f32[16,96,128]...) custom-call(f32[18,8,128]{2,1,0:T(8,128)S(1)} %get-tuple-element.25., ...), custom_call_target="tpu_custom_call", output_to_operand_aliasing={{4}: (3, {}), {5}: (4, {}), {6}: (5, {})} | custom-call | flops 16000000 | bytes 4000000 | tf_op jit(solution)/shard_map/block/pallas_call | solution.py:660
  15.1 1.1 %collective-permute-done.2.pb_ref = f32[88,128]{1,0:T(8,128)S(1)} collective-permute-done((f32[88,128]{1,0:T(8,128)S(1)}, f32[88,128]{1,0:T(8,128)S(1)}, u32[]{:S(2)}, u32[]{:S(2)}) %collective-permute-start.2) | collective-permute-done | bytes 45088 | tf_op jit(solution)/shard_map/ppermute | solution.py:614
  16.2 0.0 collective-permute-done.3.pa_ref
  16.2 1.8 %sides.1 = (f32[2,4,80,128]{3,2,1,0:T(8,128)S(1)}, f32[2,10,96,128]{3,2,1,0:T(8,128)S(1)}, f32[32,128]{1,0:T(8,128)S(1)}) custom-call(f32[18,8,128]{2,1,0:T(8,128)S(1)} %get-tuple-element.25.c_ref, f32[6,80,128]{2,1,0:T(8,128)S(1)} %get-tuple-element.38.own_ref, f32[88,128]{1,0:T(8,128)S(1)} %collective-permute-done.2.pb_ref, ...), custom_call_target="tpu_custom_call" | custom-call | tf_op jit(solution)/shard_map/sides/pallas_call | solution.py:674
  18.0 10.4 %all_to_all.11 = f32[32,1,128]{2,1,0:T(1,128)S(1)} all-to-all(f32[32,1,128]{2,1,0:T(1,128)S(1)} %bitcast.9), channel_id=1, replica_groups=mesh['lon'=8,'lat'=4] {'lon','lat'}, dimensions={0} | all-to-all | bytes 32768 | tf_op jit(solution)/shard_map/all_to_all | solution.py:687
  28.4 2.9 %finish.1 = (f32[16,64,128]{2,1,0:T(8,128)}, f32[64,128]{1,0:T(8,128)}) custom-call(f32[18,8,128]{2,1,0:T(8,128)S(1)} %get-tuple-element.25.c_ref, bf16[2,8,64,128]{3,2,1,0:T(8,128)(2,1)S(1)} %copy-done, bf16[2,8,64,128]{3,2,1,0:T(8,128)(2,1)S(1)} %copy-done.1, f32[16,80,128]{2,1,0:T(8,128)S(1)} %get-tuple-element.31.am_ref, ...), custom_call_target="tpu_custom_call" | custom-call | tf_op jit(solution)/shard_map/finish/pallas_call | solution.py:688
  (3 shorter events, 0.0 us)
Async XLA Ops:
  0.6 6.8 %copy-start = (bf16[2,8,64,128]{3,2,1,0:T(8,128)(2,1)S(1)}, bf16[2,8,64,128]{3,2,1,0:T(8,128)(2,1)}, u32[]{:S(2)}) copy-start(bf16[2,8,64,128]{3,2,1,0:T(8,128)(2,1)} %zon_ref.3) | copy-start | bytes 786436
  0.6 6.8 %copy-start.1 = (bf16[2,8,64,128]{3,2,1,0:T(8,128)(2,1)S(1)}, bf16[2,8,64,128]{3,2,1,0:T(8,128)(2,1)}, u32[]{:S(2)}) copy-start(bf16[2,8,64,128]{3,2,1,0:T(8,128)(2,1)} %mer_ref.3) | copy-start | bytes 786436
  0.7 6.7 %copy-start.2 = (f32[2,8,64,128]{3,2,1,0:T(8,128)S(1)}, f32[2,8,64,128]{3,2,1,0:T(8,128)}, u32[]{:S(2)}) copy-start(f32[2,8,64,128]{3,2,1,0:T(8,128)} %param.6) | copy-start | bytes 1572868
  0.7 6.7 %copy-start.3 = (s32[64,128]{1,0:T(8,128)S(1)}, s32[64,128]{1,0:T(8,128)}, u32[]{:S(2)}) copy-start(s32[64,128]{1,0:T(8,128)} %depth.1) | copy-start | bytes 98308
  0.7 6.7 %copy-start.4 = (f32[64,128]{1,0:T(8,128)S(1)}, f32[64,128]{1,0:T(8,128)}, u32[]{:S(2)}) copy-start(f32[64,128]{1,0:T(8,128)} %diag.1) | copy-start | bytes 98308
  1.8 5.6 %copy-start.5 = (f32[2,8]{1,0:T(2,128)S(1)}, f32[2,8]{1,0:T(2,128)}, u32[]{:S(2)}) copy-start(f32[2,8]{1,0:T(2,128)} %c_ref.1) | copy-start | bytes 196
  1.8 8.0 %collective-permute-start = (f32[120,128]{1,0:T(8,128)S(1)}, f32[120,128]{1,0:T(8,128)S(1)}, u32[]{:S(2)}, u32[]{:S(2)}) collective-permute-start(f32[120,128]{1,0:T(8,128)S(1)} %get-tuple-element.26), channel_id=1, source_target_pairs={{0,1},{1,0},{2,3},{3,2},{4,5},{5,4},{6,7},{7,6},{8,9},{9,8},{10,11... | collective-permute-start | bytes 184328 | tf_op jit(solution)/shard_map/ppermute | solution.py:614
  4.9 6.0 %collective-permute-start.1 = (f32[120,128]{1,0:T(8,128)S(1)}, f32[120,128]{1,0:T(8,128)S(1)}, u32[]{:S(2)}, u32[]{:S(2)}) collective-permute-start(f32[120,128]{1,0:T(8,128)S(1)} %get-tuple-element.27), channel_id=1, source_target_pairs={{0,3},{1,2},{2,1},{3,0},{4,7},{5,6},{6,5},{7,4},{8,11},{9,10},{10,... | collective-permute-start | bytes 184328 | tf_op jit(solution)/shard_map/ppermute | solution.py:614
  11.4 4.8 %collective-permute-start.2 = (f32[88,128]{1,0:T(8,128)S(1)}, f32[88,128]{1,0:T(8,128)S(1)}, u32[]{:S(2)}, u32[]{:S(2)}) collective-permute-start(f32[88,128]{1,0:T(8,128)S(1)} %get-tuple-element.39), channel_id=1, source_target_pairs={{0,28},{4,8},{8,4},{12,16},{16,12},{20,24},{24,20},{28,0},{1,29},{... | collective-permute-start | bytes 135176 | tf_op jit(solution)/shard_map/ppermute | solution.py:614
  12.5 3.7 %collective-permute-start.3 = (f32[88,128]{1,0:T(8,128)S(1)}, f32[88,128]{1,0:T(8,128)S(1)}, u32[]{:S(2)}, u32[]{:S(2)}) collective-permute-start(f32[88,128]{1,0:T(8,128)S(1)} %get-tuple-element.40), channel_id=1, source_target_pairs={{0,4},{4,0},{8,12},{12,8},{16,20},{20,16},{24,28},{28,24},{1,5},{5... | collective-permute-start | bytes 135176 | tf_op jit(solution)/shard_map/ppermute | solution.py:614
